TPU v7x, 256 devices: a whole 4x4x8 slice. The times are simulated.
256 devices in a mesh: depth: 4 (over x_hi, core), tile: 64 (over x_lo, y, z).
Axes of the slice: x: 4 (x_hi: 2, x_lo: 2; x = x_hi * 2 + x_lo), y: 4, z: 8, core: 2. Of those that a mesh axis runs over, the one named last changes fastest.
Arguments:
- incident: float32 [2, 3, 2048, 512], P(None, None, 'tile'), may hold values from -6 to 6
- delta: float32 [3, 8, 2048, 512], P(None, 'depth', 'tile'), may hold values from 0 to 1
- beta: float32 [3, 8, 2048, 512], P(None, 'depth', 'tile'), may hold values from 0 to 0.5
- view_order: int32 [3], replicated, may hold values from 0 to 2, each once
Outputs:
- slab_waves: float32 [2, 3, 4, 2048, 512], P(None, None, 'depth', 'tile')
Inputs may be any that keep to these rules, and one draw needn't show every extreme that they name: `view_order`: each view appears once.
All inputs are finite; a program needn't handle non-finite values.
Results may differ from a plain program's by a relative error of at most 0.0001.
Values sent between devices are 32-bit elements; how exact they have to be, the bound alone decides.
No kernel may reach another device: no remote copies, remote signals or barrier semaphores. Data moves between devices by JAX's collectives and lax.ppermute only.
A program may use at most 64 MiB of HBM per device.

v0:
```python
import jax
import jax.numpy as jnp
from jax import lax
from jax.sharding import PartitionSpec as P

HALF = 32
COL_BLOCK = 256


def padded_2(block, sides, width):
    for axis, dim in sides:
        count = lax.axis_size(axis)
        forward = [(i, i + 1) for i in range(count - 1)]
        backward = [(target, source) for source, target in forward]
        low = lax.ppermute(
            lax.slice_in_dim(block, block.shape[dim] - width, None, axis=dim), axis, forward
        )
        high = lax.ppermute(lax.slice_in_dim(block, 0, width, axis=dim), axis, backward)
        block = jnp.concatenate([low, block, high], axis=dim)
    return block


def passed_along(value, axis, steps):
    count = lax.axis_size(axis)
    first, last = (max(0, -steps), min(count, count - steps))
    return lax.ppermute(value, axis, [(source, source + steps) for source in range(first, last)])


def tap_values(offset, half):
    grid = jnp.arange(-half, half + 1).astype(jnp.float32)
    window = 0.75 + 0.25 * jnp.cos(jnp.pi * grid / (half + 1))
    angle = jnp.pi * grid * grid / (6.25 * half)
    norm = jnp.sqrt(jnp.sum(window * jnp.cos(angle)) ** 2 + jnp.sum(window * jnp.sin(angle)) ** 2)
    place = offset.astype(jnp.float32)
    inside = jnp.abs(offset) <= half
    shape_win = 0.75 + 0.25 * jnp.cos(jnp.pi * place / (half + 1))
    turn = jnp.pi * place * place / (6.25 * half)
    real_part = jnp.where(inside, shape_win * jnp.cos(turn), 0.0) / norm
    imag_part = jnp.where(inside, shape_win * jnp.sin(turn), 0.0) / norm
    return (real_part, imag_part)


def column_matrix(block, half):
    source = lax.broadcasted_iota(jnp.int32, (block + 2 * half, block), 0)
    target = lax.broadcasted_iota(jnp.int32, (block + 2 * half, block), 1)
    real_part, imag_part = tap_values(source - half - target, half)
    upper = jnp.concatenate([real_part, imag_part], axis=1)
    lower = jnp.concatenate([-imag_part, real_part], axis=1)
    return jnp.concatenate([upper, lower], axis=0)


def row_matrix(rows, half):
    target = lax.broadcasted_iota(jnp.int32, (rows, rows + 2 * half), 0)
    source = lax.broadcasted_iota(jnp.int32, (rows, rows + 2 * half), 1)
    real_part, imag_part = tap_values(source - half - target, half)
    upper = jnp.concatenate([real_part, -imag_part], axis=1)
    lower = jnp.concatenate([imag_part, real_part], axis=1)
    return jnp.concatenate([upper, lower], axis=0)


def blur_columns(field, cmat, block, half):
    width = field.shape[-1]
    padded = jnp.pad(field, ((0, 0), (0, 0), (0, 0), (half, half)))
    windows = jnp.stack(
        [padded[..., b * block : b * block + block + 2 * half] for b in range(width // block)],
        axis=3,
    )
    joined = jnp.concatenate([windows[0], windows[1]], axis=-1)
    result = jnp.dot(
        joined, cmat, precision=lax.Precision.HIGHEST, preferred_element_type=jnp.float32
    )
    lead = field.shape[1:3]
    real_part = result[..., :block].reshape(lead + (width,))
    imag_part = result[..., block:].reshape(lead + (width,))
    return jnp.stack([real_part, imag_part])


def blur_rows(wide, rmat):
    stacked = jnp.concatenate([wide[0], wide[1]], axis=1)
    result = jnp.einsum(
        "oi,vic->voc",
        rmat,
        stacked,
        precision=lax.Precision.HIGHEST,
        preferred_element_type=jnp.float32,
    )
    rows = rmat.shape[0] // 2
    return jnp.stack([result[:, :rows], result[:, rows:]])


def with_rims(field, half):
    return padded_2(field, (("tile", 2),), half)


def propagate(field, slab_delta, slab_beta, cmat, rmat, block, half):
    for piece in range(slab_delta.shape[1]):
        amp = jnp.exp(-slab_beta[:, piece])
        phase = -jnp.pi * slab_delta[:, piece]
        trans_re = amp * jnp.cos(phase)
        trans_im = amp * jnp.sin(phase)
        field = jnp.stack(
            [field[0] * trans_re - field[1] * trans_im, field[0] * trans_im + field[1] * trans_re]
        )
        wide = blur_rows(with_rims(field, half), rmat)
        field = blur_columns(wide, cmat, block, half)
    return field


def per_device(incident, delta, beta, view_order):
    half = HALF
    block = COL_BLOCK
    views = incident.shape[1]
    rows = incident.shape[2]
    cmat = column_matrix(block, half)
    rmat = row_matrix(rows, half)
    section = lax.axis_index("depth")
    sections = lax.axis_size("depth")
    slab_out = jnp.zeros((2, views, 1) + incident.shape[2:], jnp.float32)
    ordered = jnp.take(incident, view_order, axis=1)
    ordered_delta = jnp.take(delta, view_order, axis=0)
    ordered_beta = jnp.take(beta, view_order, axis=0)
    state = ordered
    for step in range(sections):
        if step > 0:
            state = passed_along(previous, "depth", 1)
        result = propagate(state, ordered_delta, ordered_beta, cmat, rmat, block, half)
        slab_out = jnp.where(section == step, result[:, :, None], slab_out)
        previous = result
    return slab_out


def solution(mesh):
    return jax.shard_map(
        per_device,
        mesh=mesh,
        in_specs=(
            P(None, None, "tile", None),
            P(None, "depth", "tile", None),
            P(None, "depth", "tile", None),
            P(),
        ),
        out_specs=P(None, None, "depth", "tile", None),
        check_vma=False,
    )
```

profile of v0, /device:TPU:6, one launch (start us, length us, event | category | flops | bytes accessed | tf_op | source)
XLA Modules:
  0.0 202.2 jit_solution(3204985512316057595)
XLA Ops:
  2.0 1.6 gather_fusion.1
  5.2 3.8 %collective-permute-start = (f32[2,3,32,512]{3,2,1,0:T(8,128)S(1)}, f32[2,3,32,512]{3,2,1,0:T(8,128)S(1)}, u32[]{:S(2)}, u32[]{:S(2)}) collective-permute-start(f32[2,3,32,512]{3,2,1,0:T(8,128)S(1)} %pad_maximum_fusion.16), channel_id=1, source_target_pairs={{0,1},{1,2},{2,3},{3,4},{4,5},{5,6},{6,7},{7,8},{8,9},{9,10},{10,1... | collective-permute-start | bytes 1179656 | tf_op jit(solution)/shard_map/ppermute | solution.py:15
  9.1 8.6 %collective-permute-start.1 = (f32[2,3,32,512]{3,2,1,0:T(8,128)S(1)}, f32[2,3,32,512]{3,2,1,0:T(8,128)S(1)}, u32[]{:S(2)}, u32[]{:S(2)}) collective-permute-start(f32[2,3,32,512]{3,2,1,0:T(8,128)S(1)} %pad_maximum_fusion.16), channel_id=1, source_target_pairs={{1,0},{2,1},{3,2},{4,3},{5,4},{6,5},{7,6},{8,7},{9,8},{10,9},{11,1... | collective-permute-start | bytes 1179656 | tf_op jit(solution)/shard_map/ppermute | solution.py:18
  21.7 2.5 %select_divide_fusion = (f32[320,256]{1,0:T(8,128)S(1)}, f32[320,256]{1,0:T(8,128)S(1)}, f32[320,256]{1,0:T(8,128)S(1)}) fusion(f32[]{:T(128)S(6)} %sqrt.4, s32[320]{0:T(512)S(1)} %iota_add_fusion), kind=kLoop, calls=%fused_computation.133 | loop fusion | flops 1392640 | bytes 984324 | tf_op jit(solution)/shard_map/div | solution.py:39
  24.8 1.2 collective-permute-done.1
  27.5 1.2 fusion.38
  30.2 1.9 collective-permute-start.2
  32.2 8.6 %collective-permute-start.3 = (f32[2,3,32,512]{3,2,1,0:T(8,128)S(1)}, f32[2,3,32,512]{3,2,1,0:T(8,128)S(1)}, u32[]{:S(2)}, u32[]{:S(2)}) collective-permute-start(f32[2,3,32,512]{3,2,1,0:T(8,128)S(1)} %pad_maximum_fusion.17), channel_id=1, source_target_pairs={{1,0},{2,1},{3,2},{4,3},{5,4},{6,5},{7,6},{8,7},{9,8},{10,9},{11,1... | collective-permute-start | bytes 1179656 | tf_op jit(solution)/shard_map/ppermute | solution.py:18
  40.8 6.3 %collective-permute-done.2 = f32[2,3,32,512]{3,2,1,0:T(8,128)S(1)} collective-permute-done((f32[2,3,32,512]{3,2,1,0:T(8,128)S(1)}, f32[2,3,32,512]{3,2,1,0:T(8,128)S(1)}, u32[]{:S(2)}, u32[]{:S(2)}) %collective-permute-start.2) | collective-permute-done | bytes 393248 | tf_op jit(solution)/shard_map/ppermute | solution.py:15
  47.1 1.2 collective-permute-done.3
  50.7 1.2 fusion.36
  52.6 1.9 collective-permute-start.4
  54.5 8.7 %collective-permute-done.4 = f32[2,3,32,512]{3,2,1,0:T(8,128)S(1)} collective-permute-done((f32[2,3,32,512]{3,2,1,0:T(8,128)S(1)}, f32[2,3,32,512]{3,2,1,0:T(8,128)S(1)}, u32[]{:S(2)}, u32[]{:S(2)}) %collective-permute-start.4) | collective-permute-done | bytes 393248 | tf_op jit(solution)/shard_map/ppermute | solution.py:26
  63.3 1.9 collective-permute-start.5
  65.2 8.8 %collective-permute-start.6 = (f32[2,3,32,512]{3,2,1,0:T(8,128)S(1)}, f32[2,3,32,512]{3,2,1,0:T(8,128)S(1)}, u32[]{:S(2)}, u32[]{:S(2)}) collective-permute-start(f32[2,3,32,512]{3,2,1,0:T(8,128)S(1)} %pad_maximum_fusion.19), channel_id=1, source_target_pairs={{1,0},{2,1},{3,2},{4,3},{5,4},{6,5},{7,6},{8,7},{9,8},{10,9},{11,1... | collective-permute-start | bytes 1179656 | tf_op jit(solution)/shard_map/ppermute | solution.py:18
  74.0 3.6 %collective-permute-done.5 = f32[2,3,32,512]{3,2,1,0:T(8,128)S(1)} collective-permute-done((f32[2,3,32,512]{3,2,1,0:T(8,128)S(1)}, f32[2,3,32,512]{3,2,1,0:T(8,128)S(1)}, u32[]{:S(2)}, u32[]{:S(2)}) %collective-permute-start.5) | collective-permute-done | bytes 393248 | tf_op jit(solution)/shard_map/ppermute | solution.py:15
  77.6 1.5 collective-permute-done.6
  80.6 1.2 fusion.34
  82.6 1.9 collective-permute-start.7
  84.5 8.6 %collective-permute-start.8 = (f32[2,3,32,512]{3,2,1,0:T(8,128)S(1)}, f32[2,3,32,512]{3,2,1,0:T(8,128)S(1)}, u32[]{:S(2)}, u32[]{:S(2)}) collective-permute-start(f32[2,3,32,512]{3,2,1,0:T(8,128)S(1)} %pad_maximum_fusion.20), channel_id=1, source_target_pairs={{1,0},{2,1},{3,2},{4,3},{5,4},{6,5},{7,6},{8,7},{9,8},{10,9},{11,1... | collective-permute-start | bytes 1179656 | tf_op jit(solution)/shard_map/ppermute | solution.py:18
  93.1 3.8 %collective-permute-done.7 = f32[2,3,32,512]{3,2,1,0:T(8,128)S(1)} collective-permute-done((f32[2,3,32,512]{3,2,1,0:T(8,128)S(1)}, f32[2,3,32,512]{3,2,1,0:T(8,128)S(1)}, u32[]{:S(2)}, u32[]{:S(2)}) %collective-permute-start.7) | collective-permute-done | bytes 393248 | tf_op jit(solution)/shard_map/ppermute | solution.py:15
  96.9 1.5 collective-permute-done.8
  99.9 1.2 fusion.32
  101.8 1.9 collective-permute-start.9
  103.7 8.7 %collective-permute-done.9 = f32[2,3,32,512]{3,2,1,0:T(8,128)S(1)} collective-permute-done((f32[2,3,32,512]{3,2,1,0:T(8,128)S(1)}, f32[2,3,32,512]{3,2,1,0:T(8,128)S(1)}, u32[]{:S(2)}, u32[]{:S(2)}) %collective-permute-start.9) | collective-permute-done | bytes 393248 | tf_op jit(solution)/shard_map/ppermute | solution.py:26
  112.5 1.9 collective-permute-start.10
  114.4 8.6 %collective-permute-start.11 = (f32[2,3,32,512]{3,2,1,0:T(8,128)S(1)}, f32[2,3,32,512]{3,2,1,0:T(8,128)S(1)}, u32[]{:S(2)}, u32[]{:S(2)}) collective-permute-start(f32[2,3,32,512]{3,2,1,0:T(8,128)S(1)} %pad_maximum_fusion.22), channel_id=1, source_target_pairs={{1,0},{2,1},{3,2},{4,3},{5,4},{6,5},{7,6},{8,7},{9,8},{10,9},{11,1... | collective-permute-start | bytes 1179656 | tf_op jit(solution)/shard_map/ppermute | solution.py:18
  123.1 3.8 %collective-permute-done.10 = f32[2,3,32,512]{3,2,1,0:T(8,128)S(1)} collective-permute-done((f32[2,3,32,512]{3,2,1,0:T(8,128)S(1)}, f32[2,3,32,512]{3,2,1,0:T(8,128)S(1)}, u32[]{:S(2)}, u32[]{:S(2)}) %collective-permute-start.10) | collective-permute-done | bytes 393248 | tf_op jit(solution)/shard_map/ppermute | solution.py:15
  126.9 1.5 collective-permute-done.11
  129.8 1.2 fusion.30
  131.8 1.9 collective-permute-start.12
  133.8 8.8 %collective-permute-start.13 = (f32[2,3,32,512]{3,2,1,0:T(8,128)S(1)}, f32[2,3,32,512]{3,2,1,0:T(8,128)S(1)}, u32[]{:S(2)}, u32[]{:S(2)}) collective-permute-start(f32[2,3,32,512]{3,2,1,0:T(8,128)S(1)} %pad_maximum_fusion.23), channel_id=1, source_target_pairs={{1,0},{2,1},{3,2},{4,3},{5,4},{6,5},{7,6},{8,7},{9,8},{10,9},{11,1... | collective-permute-start | bytes 1179656 | tf_op jit(solution)/shard_map/ppermute | solution.py:18
  142.6 3.6 %collective-permute-done.12 = f32[2,3,32,512]{3,2,1,0:T(8,128)S(1)} collective-permute-done((f32[2,3,32,512]{3,2,1,0:T(8,128)S(1)}, f32[2,3,32,512]{3,2,1,0:T(8,128)S(1)}, u32[]{:S(2)}, u32[]{:S(2)}) %collective-permute-start.12) | collective-permute-done | bytes 393248 | tf_op jit(solution)/shard_map/ppermute | solution.py:15
  146.2 1.5 collective-permute-done.13
  149.2 1.2 fusion.28
  151.1 1.9 collective-permute-start.14
  153.0 8.7 %collective-permute-done.14 = f32[2,3,32,512]{3,2,1,0:T(8,128)S(1)} collective-permute-done((f32[2,3,32,512]{3,2,1,0:T(8,128)S(1)}, f32[2,3,32,512]{3,2,1,0:T(8,128)S(1)}, u32[]{:S(2)}, u32[]{:S(2)}) %collective-permute-start.14) | collective-permute-done | bytes 393248 | tf_op jit(solution)/shard_map/ppermute | solution.py:26
  161.8 1.9 collective-permute-start.15
  163.7 8.6 %collective-permute-start.16 = (f32[2,3,32,512]{3,2,1,0:T(8,128)S(1)}, f32[2,3,32,512]{3,2,1,0:T(8,128)S(1)}, u32[]{:S(2)}, u32[]{:S(2)}) collective-permute-start(f32[2,3,32,512]{3,2,1,0:T(8,128)S(1)} %pad_maximum_fusion.25), channel_id=1, source_target_pairs={{1,0},{2,1},{3,2},{4,3},{5,4},{6,5},{7,6},{8,7},{9,8},{10,9},{11,1... | collective-permute-start | bytes 1179656 | tf_op jit(solution)/shard_map/ppermute | solution.py:18
  172.3 3.8 %collective-permute-done.15 = f32[2,3,32,512]{3,2,1,0:T(8,128)S(1)} collective-permute-done((f32[2,3,32,512]{3,2,1,0:T(8,128)S(1)}, f32[2,3,32,512]{3,2,1,0:T(8,128)S(1)}, u32[]{:S(2)}, u32[]{:S(2)}) %collective-permute-start.15) | collective-permute-done | bytes 393248 | tf_op jit(solution)/shard_map/ppermute | solution.py:15
  176.2 1.5 collective-permute-done.16
  179.1 1.2 fusion.26
  181.1 1.9 collective-permute-start.17
  183.1 8.6 %collective-permute-start.18 = (f32[2,3,32,512]{3,2,1,0:T(8,128)S(1)}, f32[2,3,32,512]{3,2,1,0:T(8,128)S(1)}, u32[]{:S(2)}, u32[]{:S(2)}) collective-permute-start(f32[2,3,32,512]{3,2,1,0:T(8,128)S(1)} %pad_maximum_fusion.26), channel_id=1, source_target_pairs={{1,0},{2,1},{3,2},{4,3},{5,4},{6,5},{7,6},{8,7},{9,8},{10,9},{11,1... | collective-permute-start | bytes 1179656 | tf_op jit(solution)/shard_map/ppermute | solution.py:18
  192.7 2.8 %collective-permute-done.17 = f32[2,3,32,512]{3,2,1,0:T(8,128)S(1)} collective-permute-done((f32[2,3,32,512]{3,2,1,0:T(8,128)S(1)}, f32[2,3,32,512]{3,2,1,0:T(8,128)S(1)}, u32[]{:S(2)}, u32[]{:S(2)}) %collective-permute-start.17) | collective-permute-done | bytes 393248 | tf_op jit(solution)/shard_map/ppermute | solution.py:15
  195.5 1.5 collective-permute-done.18
  199.4 1.2 fusion.24
  201.3 0.9 fusion.41
  (151 shorter events, 26.8 us)
Async XLA Ops:
  0.0 1.4 copy-start
  0.0 3.6 %copy-start.2 = (f32[3,2,32,512]{3,2,1,0:T(8,128)S(1)}, f32[3,2,32,512]{3,2,1,0:T(8,128)}, u32[]{:S(2)}) copy-start(f32[3,2,32,512]{3,2,1,0:T(8,128)} %param.7) | copy-start | bytes 1179652
  5.2 19.6 %collective-permute-start = (f32[2,3,32,512]{3,2,1,0:T(8,128)S(1)}, f32[2,3,32,512]{3,2,1,0:T(8,128)S(1)}, u32[]{:S(2)}, u32[]{:S(2)}) collective-permute-start(f32[2,3,32,512]{3,2,1,0:T(8,128)S(1)} %pad_maximum_fusion.16), channel_id=1, source_target_pairs={{0,1},{1,2},{2,3},{3,4},{4,5},{5,6},{6,7},{7,8},{8,9},{9,10},{10,1... | collective-permute-start | bytes 1179656 | tf_op jit(solution)/shard_map/ppermute | solution.py:15
  9.1 16.9 %collective-permute-start.1 = (f32[2,3,32,512]{3,2,1,0:T(8,128)S(1)}, f32[2,3,32,512]{3,2,1,0:T(8,128)S(1)}, u32[]{:S(2)}, u32[]{:S(2)}) collective-permute-start(f32[2,3,32,512]{3,2,1,0:T(8,128)S(1)} %pad_maximum_fusion.16), channel_id=1, source_target_pairs={{1,0},{2,1},{3,2},{4,3},{5,4},{6,5},{7,6},{8,7},{9,8},{10,9},{11,1... | collective-permute-start | bytes 1179656 | tf_op jit(solution)/shard_map/ppermute | solution.py:18
  24.2 3.3 %copy-start.5 = (f32[320,256]{1,0:T(8,128)}, f32[320,256]{1,0:T(8,128)S(1)}, u32[]{:S(2)}) copy-start(f32[320,256]{1,0:T(8,128)S(1)} %get-tuple-element.106) | copy-start | bytes 983044
  24.2 154.9 %copy-start.3 = (f32[320,256]{1,0:T(8,128)}, f32[320,256]{1,0:T(8,128)S(1)}, u32[]{:S(2)}) copy-start(f32[320,256]{1,0:T(8,128)S(1)} %get-tuple-element.105) | copy-start | bytes 983044
  30.2 16.9 %collective-permute-start.2 = (f32[2,3,32,512]{3,2,1,0:T(8,128)S(1)}, f32[2,3,32,512]{3,2,1,0:T(8,128)S(1)}, u32[]{:S(2)}, u32[]{:S(2)}) collective-permute-start(f32[2,3,32,512]{3,2,1,0:T(8,128)S(1)} %pad_maximum_fusion.17), channel_id=1, source_target_pairs={{0,1},{1,2},{2,3},{3,4},{4,5},{5,6},{6,7},{7,8},{8,9},{9,10},{10,1... | collective-permute-start | bytes 1179656 | tf_op jit(solution)/shard_map/ppermute | solution.py:15
  32.2 16.1 %collective-permute-start.3 = (f32[2,3,32,512]{3,2,1,0:T(8,128)S(1)}, f32[2,3,32,512]{3,2,1,0:T(8,128)S(1)}, u32[]{:S(2)}, u32[]{:S(2)}) collective-permute-start(f32[2,3,32,512]{3,2,1,0:T(8,128)S(1)} %pad_maximum_fusion.17), channel_id=1, source_target_pairs={{1,0},{2,1},{3,2},{4,3},{5,4},{6,5},{7,6},{8,7},{9,8},{10,9},{11,1... | collective-permute-start | bytes 1179656 | tf_op jit(solution)/shard_map/ppermute | solution.py:18
  49.7 1.0 copy-start.6
  52.6 10.6 %collective-permute-start.4 = (f32[2,3,32,512]{3,2,1,0:T(8,128)S(1)}, f32[2,3,32,512]{3,2,1,0:T(8,128)S(1)}, u32[]{:S(2)}, u32[]{:S(2)}) collective-permute-start(f32[2,3,32,512]{3,2,1,0:T(8,128)S(1)} %pad_maximum_fusion.18), channel_id=1, source_target_pairs={{0,64},{64,128},{128,192},{1,65},{65,129},{129,193},{2,66},{66,130... | collective-permute-start | bytes 1179656 | tf_op jit(solution)/shard_map/ppermute | solution.py:26
  63.3 14.4 %collective-permute-start.5 = (f32[2,3,32,512]{3,2,1,0:T(8,128)S(1)}, f32[2,3,32,512]{3,2,1,0:T(8,128)S(1)}, u32[]{:S(2)}, u32[]{:S(2)}) collective-permute-start(f32[2,3,32,512]{3,2,1,0:T(8,128)S(1)} %pad_maximum_fusion.19), channel_id=1, source_target_pairs={{0,1},{1,2},{2,3},{3,4},{4,5},{5,6},{6,7},{7,8},{8,9},{9,10},{10,1... | collective-permute-start | bytes 1179656 | tf_op jit(solution)/shard_map/ppermute | solution.py:15
  65.2 13.9 %collective-permute-start.6 = (f32[2,3,32,512]{3,2,1,0:T(8,128)S(1)}, f32[2,3,32,512]{3,2,1,0:T(8,128)S(1)}, u32[]{:S(2)}, u32[]{:S(2)}) collective-permute-start(f32[2,3,32,512]{3,2,1,0:T(8,128)S(1)} %pad_maximum_fusion.19), channel_id=1, source_target_pairs={{1,0},{2,1},{3,2},{4,3},{5,4},{6,5},{7,6},{8,7},{9,8},{10,9},{11,1... | collective-permute-start | bytes 1179656 | tf_op jit(solution)/shard_map/ppermute | solution.py:18
  82.6 14.4 %collective-permute-start.7 = (f32[2,3,32,512]{3,2,1,0:T(8,128)S(1)}, f32[2,3,32,512]{3,2,1,0:T(8,128)S(1)}, u32[]{:S(2)}, u32[]{:S(2)}) collective-permute-start(f32[2,3,32,512]{3,2,1,0:T(8,128)S(1)} %pad_maximum_fusion.20), channel_id=1, source_target_pairs={{0,1},{1,2},{2,3},{3,4},{4,5},{5,6},{6,7},{7,8},{8,9},{9,10},{10,1... | collective-permute-start | bytes 1179656 | tf_op jit(solution)/shard_map/ppermute | solution.py:15
  84.5 13.9 %collective-permute-start.8 = (f32[2,3,32,512]{3,2,1,0:T(8,128)S(1)}, f32[2,3,32,512]{3,2,1,0:T(8,128)S(1)}, u32[]{:S(2)}, u32[]{:S(2)}) collective-permute-start(f32[2,3,32,512]{3,2,1,0:T(8,128)S(1)} %pad_maximum_fusion.20), channel_id=1, source_target_pairs={{1,0},{2,1},{3,2},{4,3},{5,4},{6,5},{7,6},{8,7},{9,8},{10,9},{11,1... | collective-permute-start | bytes 1179656 | tf_op jit(solution)/shard_map/ppermute | solution.py:18
  101.8 10.6 %collective-permute-start.9 = (f32[2,3,32,512]{3,2,1,0:T(8,128)S(1)}, f32[2,3,32,512]{3,2,1,0:T(8,128)S(1)}, u32[]{:S(2)}, u32[]{:S(2)}) collective-permute-start(f32[2,3,32,512]{3,2,1,0:T(8,128)S(1)} %pad_maximum_fusion.21), channel_id=1, source_target_pairs={{0,64},{64,128},{128,192},{1,65},{65,129},{129,193},{2,66},{66,130... | collective-permute-start | bytes 1179656 | tf_op jit(solution)/shard_map/ppermute | solution.py:26
  112.5 14.4 %collective-permute-start.10 = (f32[2,3,32,512]{3,2,1,0:T(8,128)S(1)}, f32[2,3,32,512]{3,2,1,0:T(8,128)S(1)}, u32[]{:S(2)}, u32[]{:S(2)}) collective-permute-start(f32[2,3,32,512]{3,2,1,0:T(8,128)S(1)} %pad_maximum_fusion.22), channel_id=1, source_target_pairs={{0,1},{1,2},{2,3},{3,4},{4,5},{5,6},{6,7},{7,8},{8,9},{9,10},{10,1... | collective-permute-start | bytes 1179656 | tf_op jit(solution)/shard_map/ppermute | solution.py:15
  114.4 13.9 %collective-permute-start.11 = (f32[2,3,32,512]{3,2,1,0:T(8,128)S(1)}, f32[2,3,32,512]{3,2,1,0:T(8,128)S(1)}, u32[]{:S(2)}, u32[]{:S(2)}) collective-permute-start(f32[2,3,32,512]{3,2,1,0:T(8,128)S(1)} %pad_maximum_fusion.22), channel_id=1, source_target_pairs={{1,0},{2,1},{3,2},{4,3},{5,4},{6,5},{7,6},{8,7},{9,8},{10,9},{11,1... | collective-permute-start | bytes 1179656 | tf_op jit(solution)/shard_map/ppermute | solution.py:18
  131.8 14.4 %collective-permute-start.12 = (f32[2,3,32,512]{3,2,1,0:T(8,128)S(1)}, f32[2,3,32,512]{3,2,1,0:T(8,128)S(1)}, u32[]{:S(2)}, u32[]{:S(2)}) collective-permute-start(f32[2,3,32,512]{3,2,1,0:T(8,128)S(1)} %pad_maximum_fusion.23), channel_id=1, source_target_pairs={{0,1},{1,2},{2,3},{3,4},{4,5},{5,6},{6,7},{7,8},{8,9},{9,10},{10,1... | collective-permute-start | bytes 1179656 | tf_op jit(solution)/shard_map/ppermute | solution.py:15
  133.8 13.9 %collective-permute-start.13 = (f32[2,3,32,512]{3,2,1,0:T(8,128)S(1)}, f32[2,3,32,512]{3,2,1,0:T(8,128)S(1)}, u32[]{:S(2)}, u32[]{:S(2)}) collective-permute-start(f32[2,3,32,512]{3,2,1,0:T(8,128)S(1)} %pad_maximum_fusion.23), channel_id=1, source_target_pairs={{1,0},{2,1},{3,2},{4,3},{5,4},{6,5},{7,6},{8,7},{9,8},{10,9},{11,1... | collective-permute-start | bytes 1179656 | tf_op jit(solution)/shard_map/ppermute | solution.py:18
  151.1 10.6 %collective-permute-start.14 = (f32[2,3,32,512]{3,2,1,0:T(8,128)S(1)}, f32[2,3,32,512]{3,2,1,0:T(8,128)S(1)}, u32[]{:S(2)}, u32[]{:S(2)}) collective-permute-start(f32[2,3,32,512]{3,2,1,0:T(8,128)S(1)} %pad_maximum_fusion.24), channel_id=1, source_target_pairs={{0,64},{64,128},{128,192},{1,65},{65,129},{129,193},{2,66},{66,130... | collective-permute-start | bytes 1179656 | tf_op jit(solution)/shard_map/ppermute | solution.py:26
  161.8 14.4 %collective-permute-start.15 = (f32[2,3,32,512]{3,2,1,0:T(8,128)S(1)}, f32[2,3,32,512]{3,2,1,0:T(8,128)S(1)}, u32[]{:S(2)}, u32[]{:S(2)}) collective-permute-start(f32[2,3,32,512]{3,2,1,0:T(8,128)S(1)} %pad_maximum_fusion.25), channel_id=1, source_target_pairs={{0,1},{1,2},{2,3},{3,4},{4,5},{5,6},{6,7},{7,8},{8,9},{9,10},{10,1... | collective-permute-start | bytes 1179656 | tf_op jit(solution)/shard_map/ppermute | solution.py:15
  163.7 13.9 %collective-permute-start.16 = (f32[2,3,32,512]{3,2,1,0:T(8,128)S(1)}, f32[2,3,32,512]{3,2,1,0:T(8,128)S(1)}, u32[]{:S(2)}, u32[]{:S(2)}) collective-permute-start(f32[2,3,32,512]{3,2,1,0:T(8,128)S(1)} %pad_maximum_fusion.25), channel_id=1, source_target_pairs={{1,0},{2,1},{3,2},{4,3},{5,4},{6,5},{7,6},{8,7},{9,8},{10,9},{11,1... | collective-permute-start | bytes 1179656 | tf_op jit(solution)/shard_map/ppermute | solution.py:18
  181.1 14.4 %collective-permute-start.17 = (f32[2,3,32,512]{3,2,1,0:T(8,128)S(1)}, f32[2,3,32,512]{3,2,1,0:T(8,128)S(1)}, u32[]{:S(2)}, u32[]{:S(2)}) collective-permute-start(f32[2,3,32,512]{3,2,1,0:T(8,128)S(1)} %pad_maximum_fusion.26), channel_id=1, source_target_pairs={{0,1},{1,2},{2,3},{3,4},{4,5},{5,6},{6,7},{7,8},{8,9},{9,10},{10,1... | collective-permute-start | bytes 1179656 | tf_op jit(solution)/shard_map/ppermute | solution.py:15
  183.1 13.9 %collective-permute-start.18 = (f32[2,3,32,512]{3,2,1,0:T(8,128)S(1)}, f32[2,3,32,512]{3,2,1,0:T(8,128)S(1)}, u32[]{:S(2)}, u32[]{:S(2)}) collective-permute-start(f32[2,3,32,512]{3,2,1,0:T(8,128)S(1)} %pad_maximum_fusion.26), channel_id=1, source_target_pairs={{1,0},{2,1},{3,2},{4,3},{5,4},{6,5},{7,6},{8,7},{9,8},{10,9},{11,1... | collective-permute-start | bytes 1179656 | tf_op jit(solution)/shard_map/ppermute | solution.py:18
  198.3 1.0 copy-start.4
  198.3 1.1 copy-start.7
  201.0 1.3 copy-start.1
where the time goes:
time: 203 us; the launch traced here: 202 us
  starting transfers between devices  92.3 us (45%)
  waiting for transfers between devices  65.5 us (32%)
  matrix products  16.7 us (8%)
  local copies, waits for them, and re-layouts  12.3 us (6%)
  other arithmetic  11.6 us (6%)
  between operations  3.83 us (2%)
    ppermute x8, starting transfers between devices, padded_2(): lax.ppermute(lax.slice_in_dim(block, 0, width, axis=dim), axis, backward)  69.2 us
    ppermute x8, waiting for transfers between devices, padded_2(): lax.ppermute(lax.slice_in_dim(block, block.shape[dim] - width, None, axis...  28.4 us
    ppermute x3, waiting for transfers between devices, passed_along(): lax.ppermute(value, axis, [(source, source + steps) for source in range(f...  26 us
    ppermute x8, starting transfers between devices, padded_2(): lax.ppermute(lax.slice_in_dim(block, block.shape[dim] - width, None, axis...  17.3 us
    ppermute x8, waiting for transfers between devices, padded_2(): lax.ppermute(lax.slice_in_dim(block, 0, width, axis=dim), axis, backward)  11.1 us
    dot_general x8, matrix products, blur_columns(): jnp.dot(joined, cmat, precision=lax.Precision.HIGHEST, preferred_element_...  9.42 us
    dot_general x8, matrix products, blur_rows(): jnp.einsum('oi,vic->voc', rmat, stacked, precision=lax.Precision.HIGHEST,...  7.26 us
    ppermute x3, starting transfers between devices, passed_along(): lax.ppermute(value, axis, [(source, source + steps) for source in range(f...  5.76 us
  transfers between devices with their start and end apart: 19, of which 19 were waited for; matrix products, arithmetic and copies ran while one was open for 2% of the time, Pallas kernels for 0%

commit v1 on v0

v1 whole, which is shorter than its diff:
```python
import jax
import jax.numpy as jnp
import numpy as np
from jax import lax
from jax.experimental import pallas as pl
from jax.experimental.pallas import tpu as pltpu
from jax.sharding import PartitionSpec as P

HALF = 32
ROWS = 32
COLS = 512
LANES = 128
VIEWS = 3
SLABS = 4
TILES = 64
AXES = ("depth", "tile")
USE_KERNELS = True


def device_at(x, y, z, core):
    return ((x // 2) * 2 + core) * TILES + (x % 2) * 32 + y * 8 + z


def worker(slot, tile):
    chip, core = divmod(tile, 2)
    x_lo, rest = divmod(chip, 16)
    y, z = divmod(rest, 4)
    z = z if y % 2 == 0 else 3 - z
    y = y if x_lo == 0 else 3 - y
    return device_at(2 * (slot // 2) + x_lo, y, z + 4 * (slot % 2), core)


def home(depth, tile):
    return depth * TILES + tile


INNER = [(worker(k, p), worker(k, p ^ 1)) for k in range(4) for p in range(TILES)]
OUTER = [
    (worker(k, p), worker(k, (p + 1) % TILES if p % 2 else (p - 1) % TILES))
    for k in range(4)
    for p in range(TILES)
]


def taps():
    grid = np.arange(-HALF, HALF + 1).astype(np.float64)
    value = (0.75 + 0.25 * np.cos(np.pi * grid / (HALF + 1))) * np.exp(1j * np.pi * grid * grid / (6.25 * HALF))
    return value / np.abs(value.sum())


def tap_at(offset):
    table = taps()
    inside = np.abs(offset) <= HALF
    return np.where(inside, table[np.clip(offset + HALF, 0, 2 * HALF)], 0.0)


def halves(matrix):
    matrix = jnp.asarray(matrix.astype(np.float32))
    high = matrix.astype(jnp.bfloat16)
    low = (matrix - high.astype(jnp.float32)).astype(jnp.bfloat16)
    return high, low


def column_matrix():
    source = np.arange(3 * LANES)[:, None] - LANES
    target = np.arange(LANES)[None, :]
    value = tap_at(source - target)
    return np.concatenate([value.real, value.imag], axis=1)


def row_block(shift):
    target = np.arange(ROWS)[:, None]
    source = np.arange(ROWS)[None, :] + shift
    value = tap_at(source - target)
    return np.block([[value.real, -value.imag], [value.imag, value.real]])


def row_matrix(parity):
    low, mid, high = row_block(-ROWS), row_block(0), row_block(ROWS)
    first, last = (low, high) if parity else (high, low)
    return np.concatenate([first, mid, last], axis=1)


def split(value):
    high = value.astype(jnp.bfloat16)
    return high, (value - high.astype(jnp.float32)).astype(jnp.bfloat16)


def dot(a, b):
    return jnp.dot(a, b, preferred_element_type=jnp.float32)


def row_blur(inner, own, outer, rhi, rlo):
    high, low = split(jnp.concatenate([inner, own, outer], axis=0))
    return dot(rhi, high) + (dot(rlo, high) + dot(rhi, low))


def column_blur(field, chi, clo):
    high, low = split(field)
    parts = []
    for b in range(COLS // LANES):
        first, last = max(0, b - 1), min(COLS // LANES, b + 2)
        cols = slice(first * LANES, last * LANES)
        rows = slice((first - b + 1) * LANES, (last - b + 1) * LANES)
        h, l = high[:, cols], low[:, cols]
        ch, cl = chi[rows], clo[rows]
        out = dot(h, ch) + (dot(l, ch) + dot(h, cl))
        real = out[:ROWS, :LANES] - out[ROWS:, LANES:]
        imag = out[:ROWS, LANES:] + out[ROWS:, :LANES]
        parts.append(jnp.concatenate([real, imag], axis=0))
    return jnp.concatenate(parts, axis=1)


def times(trans, field):
    tr, ti = trans[:ROWS], trans[ROWS:]
    fr, fi = field[:ROWS], field[ROWS:]
    return jnp.concatenate([fr * tr - fi * ti, fr * ti + fi * tr], axis=0)


def sin_poly(x):
    s = x * x
    p = -2.5052108385441720e-08
    for c in (2.7557319223985893e-06, -1.9841269841269841e-04, 8.3333333333333333e-03, -1.6666666666666667e-01):
        p = p * s + c
    return x + x * (s * p)


def cos_poly(x):
    s = x * x
    p = 2.0876756987868099e-09
    for c in (-2.7557319223985888e-07, 2.4801587301587302e-05, -1.3888888888888889e-03, 4.1666666666666667e-02, -0.5):
        p = p * s + c
    return 1.0 + s * p


def transmission(delta, beta):
    turn = (delta - 0.5) * np.float32(np.pi)
    amp = jnp.exp(-beta)
    return jnp.concatenate([-amp * sin_poly(turn), -amp * cos_poly(turn)], axis=0)


def pick(index, values):
    out = values[0]
    for i in range(1, len(values)):
        out = jnp.where(index == i, values[i], out)
    return out


def prepare_kernel(order, incident, delta, beta, *outs):
    depth = order[3]
    for slot in range(VIEWS):
        view = order[slot]
        even = transmission(delta[view, 0], beta[view, 0])
        odd = transmission(delta[view, 1], beta[view, 1])
        entering = jnp.concatenate([incident[0, view], incident[1, view]], axis=0)
        outs[slot][...] = times(even, entering)
        outs[VIEWS + slot][...] = odd
        place = lax.rem(depth + 5 - slot, 3)
        outs[2 * VIEWS][place, 0] = even
        outs[2 * VIEWS][place, 1] = odd


def first_kernel(a, b, c, chi, clo, out):
    out[...] = column_blur(a[...] + b[...] + c[...], chi[...], clo[...])


def middle_kernel(slab_end, n_trans, which, inner, own, outer, *refs):
    trans = refs[:n_trans]
    rhi, rlo, chi, clo = refs[n_trans : n_trans + 4]
    outs = refs[n_trans + 4 :]
    field = row_blur(inner[...], own[...], outer[...], rhi[...], rlo[...])
    if slab_end:
        outs[1][...] = field
    t = pick(which[0], [r[...] for r in trans])
    outs[0][...] = column_blur(times(t, field), chi[...], clo[...])


def last_kernel(inner, own, outer, rhi, rlo, out):
    out[...] = row_blur(inner[...], own[...], outer[...], rhi[...], rlo[...])


FIELD = jax.ShapeDtypeStruct((2 * ROWS, COLS), jnp.float32)


def call(kernel, out_shape, args, name, scalar_first=False):
    vmem = pl.BlockSpec(memory_space=pltpu.VMEM)
    smem = pl.BlockSpec(memory_space=pltpu.SMEM)
    specs = [smem if scalar_first and i == 0 else vmem for i in range(len(args))]
    outs = jax.tree.map(lambda _: vmem, out_shape)
    return pl.pallas_call(
        kernel, out_shape=out_shape, in_specs=specs, out_specs=outs, name=name, interpret=not USE_KERNELS
    )(*args)


def permute(value, pairs):
    return lax.ppermute(value, AXES, pairs)


def per_device(incident, delta, beta, view_order):
    depth, tile = lax.axis_index("depth"), lax.axis_index("tile")
    core = depth % 2
    slot = (depth // 2) * 2 + (tile % 8) // 4

    chi, clo = halves(column_matrix())
    even, odd = row_matrix(0), row_matrix(1)
    edge = jnp.logical_or(
        jnp.logical_and(core == 0, tile % 32 // 8 + tile // 32 * 4 + tile % 4 == 0),
        jnp.logical_and(core == 1, jnp.logical_and(tile // 32 == 1, tile % 32 // 8 + tile % 4 == 0)),
    )
    keep = jnp.logical_or(jnp.logical_not(edge), jnp.arange(6 * ROWS)[None, :] < 4 * ROWS)
    (ehi, elo), (ohi, olo) = halves(even), halves(odd)
    rhi = jnp.where(keep, jnp.where(core == 0, ehi, ohi), 0)
    rlo = jnp.where(keep, jnp.where(core == 0, elo, olo), 0)

    scalars = jnp.concatenate([view_order, depth[None]])
    pair = jax.ShapeDtypeStruct((VIEWS, 2) + FIELD.shape, jnp.float32)
    sent = call(
        prepare_kernel, [FIELD] * (2 * VIEWS) + [pair], (scalars, incident, delta, beta), "prepare", scalar_first=True
    )
    entering, second, rest = sent[:VIEWS], sent[VIEWS : 2 * VIEWS], sent[2 * VIEWS]

    def from_first(values):
        return [
            permute(values[k], [(home(0, p), worker(k, p)) for p in range(TILES)]) for k in range(VIEWS)
        ]

    starts = from_first(entering)
    seconds = from_first(second)
    later = [
        permute(
            rest[m],
            [(home(1 + (m + k) % 3, p), worker(k, p)) for k in range(VIEWS) for p in range(TILES)],
        )
        for m in range(3)
    ]

    own = call(first_kernel, FIELD, (*starts, chi, clo), "enter")
    slabs = []
    for piece in range(2 * SLABS):
        inner = permute(own, INNER)
        outer = permute(own, OUTER)
        if piece == 2 * SLABS - 1:
            slabs.append(call(last_kernel, FIELD, (inner, own, outer, rhi, rlo), "leave"))
            break
        nxt = piece + 1
        if nxt == 1:
            trans = list(seconds)
            which = jnp.minimum(slot, 2)[None]
        else:
            trans = [v[nxt % 2] for v in later]
            which = ((nxt // 2 + 5 - jnp.minimum(slot, 2)) % 3)[None]
        slab_end = piece % 2 == 1
        outs = call(
            lambda *refs, slab_end=slab_end, n=len(trans): middle_kernel(slab_end, n, *refs),
            [FIELD] * (2 if slab_end else 1),
            (which, inner, own, outer, *trans, rhi, rlo, chi, clo),
            "slice",
            scalar_first=True,
        )
        own = outs[0]
        if slab_end:
            slabs.append(outs[1])

    early = [
        permute(
            pick((slot + n) % 3, slabs[:3]),
            [(worker(k, p), home((n + k) % 3, p)) for k in range(VIEWS) for p in range(TILES)],
        )
        for n in range(3)
    ]
    last = [permute(slabs[3], [(worker(k, p), home(3, p)) for p in range(TILES)]) for k in range(VIEWS)]
    stored = [jnp.where(depth == 3, last[k], pick((depth + 3 - k) % 3, early)) for k in range(VIEWS)]
    return jnp.stack([v.reshape(2, ROWS, COLS) for v in stored], axis=1)[:, :, None]


def solution(mesh):
    return jax.shard_map(
        per_device,
        mesh=mesh,
        in_specs=(
            P(None, None, "tile", None),
            P(None, "depth", "tile", None),
            P(None, "depth", "tile", None),
            P(),
        ),
        out_specs=P(None, None, "depth", "tile", None),
        check_vma=False,
    )
```

time: 203 us -> 152 us (0.75)
  the two profiles are of different devices: /device:TPU:6 before, /device:TPU:7 now
where the time goes in v1:
time: 152 us; the launch traced here: 151 us
  starting transfers between devices  72.7 us (48%)
  waiting for transfers between devices  40 us (26%)
  Pallas kernels  25.5 us (17%)
  local copies, waits for them, and re-layouts  9.97 us (7%)
  other arithmetic  2.18 us (1%)
    ppermute x31, starting transfers between devices, permute(): return lax.ppermute(value, AXES, pairs)  72.7 us
    ppermute x31, waiting for transfers between devices, permute(): return lax.ppermute(value, AXES, pairs)  40 us
    pallas_call x10, Pallas kernels, call(): pl.pallas_call(kernel, out_shape=out_shape, in_specs=specs, out_specs=out...  25.5 us
    unnamed x62, local copies, waits for them, and re-layouts  6.65 us
  transfers between devices with their start and end apart: 31, of which 11 were waited for; matrix products, arithmetic and copies ran while one was open for 3% of the time, Pallas kernels for 5%

profile of v1, /device:TPU:7, one launch (start us, length us, event | category | flops | bytes accessed | tf_op | source)
XLA Modules:
  0.0 150.9 jit_solution(6201269295364296145)
XLA Ops:
  1.3 2.7 %prepare.1 = (f32[64,512]{1,0:T(8,128)}, f32[64,512]{1,0:T(8,128)}, f32[64,512]{1,0:T(8,128)}, f32[64,512]{1,0:T(8,128)}, f32[64,512]{1,0:T(8,128)}, /*index=5*/f32[64,512]{1,0:T(8,128)}, f32[3,2,64,512]{3,2,1,0:T(8,128)}) custom-call(s32[4]{0:T(128)} %pad_add_fusion.order, f32[2,3,32,512]{3,2,1,0:T(8,128)} %incident.1, f32[3,2,32,512]{3,2,1,0:T(8,128)} %delta.1, ...), custom_call_target="tpu_custom_call" | custom-call | tf_op jit(solution)/shard_map/prepare/pallas_call | solution.py:190
  4.6 0.7 collective-permute-start.1
  5.3 1.3 collective-permute-start.2
  6.6 0.7 collective-permute-start.5
  7.3 0.7 collective-permute-start.6
  8.0 1.2 slice_bitcast_fusion
  9.3 19.3 %collective-permute-start.12 = (f32[2,64,512]{2,1,0:T(8,128)S(1)}, f32[2,64,512]{2,1,0:T(8,128)S(1)}, u32[]{:S(2)}, u32[]{:S(2)}) collective-permute-start(f32[2,64,512]{2,1,0:T(8,128)S(1)} %get-tuple-element.31), channel_id=1, source_target_pairs={{192,0},{193,64},{194,1},{195,65},{196,2},{197,66},{198,3},{199,67... | collective-permute-start | bytes 786440 | tf_op jit(solution)/shard_map/ppermute | solution.py:196
  28.6 1.3 collective-permute-start.7
  29.9 5.2 %collective-permute-start.11 = (f32[2,64,512]{2,1,0:T(8,128)S(1)}, f32[2,64,512]{2,1,0:T(8,128)S(1)}, u32[]{:S(2)}, u32[]{:S(2)}) collective-permute-start(f32[2,64,512]{2,1,0:T(8,128)S(1)} %get-tuple-element.32), channel_id=1, source_target_pairs={{128,0},{129,64},{130,1},{131,65},{132,2},{133,66},{134,3},{135,67... | collective-permute-start | bytes 786440 | tf_op jit(solution)/shard_map/ppermute | solution.py:196
  35.1 2.3 %enter.1.refs_2_ = f32[64,512]{1,0:T(8,128)} custom-call(f32[64,512]{1,0:T(8,128)} %copy-done.2, f32[64,512]{1,0:T(8,128)} %copy-done.3, f32[64,512]{1,0:T(8,128)} %copy-done.4, bf16[384,256]{1,0:T(8,128)(2,1)} %constant.149.chi.refs_9_, bf16[384,256]{1,0:T(8,128)(2,1)} %constant.152.clo.refs_10_), custom_call_target="tpu_custom_call" | custom-call | tf_op jit(solution)/shard_map/enter/pallas_call | solution.py:190
  38.6 7.0 %collective-permute-done.7.refs_6_ = f32[64,512]{1,0:T(8,128)S(1)} collective-permute-done((f32[64,512]{1,0:T(8,128)S(1)}, f32[64,512]{1,0:T(8,128)S(1)}, u32[]{:S(2)}, u32[]{:S(2)}) %collective-permute-start.7) | collective-permute-done | bytes 131104 | tf_op jit(solution)/shard_map/ppermute | solution.py:196
  45.7 1.9 %collective-permute-start.10 = (f32[2,64,512]{2,1,0:T(8,128)S(1)}, f32[2,64,512]{2,1,0:T(8,128)S(1)}, u32[]{:S(2)}, u32[]{:S(2)}) collective-permute-start(f32[2,64,512]{2,1,0:T(8,128)S(1)} %get-tuple-element.33), channel_id=1, source_target_pairs={{64,0},{65,64},{66,1},{67,65},{68,2},{69,66},{70,3},{71,67},{72,11... | collective-permute-start | bytes 786440 | tf_op jit(solution)/shard_map/ppermute | solution.py:196
  48.3 2.7 %slice.70.refs_2_ = f32[64,512]{1,0:T(8,128)} custom-call(s32[1]{0:T(128)} %bitcast.3.refs_0_, f32[64,512]{1,0:T(8,128)} %copy-done.6, f32[64,512]{1,0:T(8,128)} %enter.1.refs_2_, f32[64,512]{1,0:T(8,128)} %copy-done.7, f32[64,512]{1,0:T(8,128)} %copy-done, f32[64,512]{1,0:T(8,128)} %copy-done.1, f32[64,512]{1,0:T(8,128)} %copy-done.5, ...), custom_call_target="tpu_custom_call" | custom-call | tf_op jit(solution)/shard_map/slice/pallas_call | solution.py:190
  51.0 2.9 %collective-permute-start.9 = (f32[64,512]{1,0:T(8,128)}, f32[64,512]{1,0:T(8,128)S(1)}, u32[]{:S(2)}, u32[]{:S(2)}) collective-permute-start(f32[64,512]{1,0:T(8,128)} %slice.70.refs_2_), channel_id=1, source_target_pairs={{0,96},{64,1},{1,64},{65,2},{2,65},{66,3},{3,66},{67,11},{11,67},{... | collective-permute-start | bytes 393224 | tf_op jit(solution)/shard_map/ppermute | solution.py:196
  53.9 0.7 slice_bitcast_fusion.3
  54.6 0.7 slice_bitcast_fusion.4
  55.3 2.2 %collective-permute-done.10 = f32[2,64,512]{2,1,0:T(8,128)S(1)} collective-permute-done((f32[2,64,512]{2,1,0:T(8,128)S(1)}, f32[2,64,512]{2,1,0:T(8,128)S(1)}, u32[]{:S(2)}, u32[]{:S(2)}) %collective-permute-start.10) | collective-permute-done | bytes 262176 | tf_op jit(solution)/shard_map/ppermute | solution.py:196
  57.5 0.7 slice_bitcast_fusion.5
  58.9 2.6 %slice.71 = (f32[64,512]{1,0:T(8,128)}, f32[64,512]{1,0:T(8,128)}) custom-call(s32[1]{0:T(128)} %bitcast.2.refs_0_, f32[64,512]{1,0:T(8,128)} %copy-done.10, f32[64,512]{1,0:T(8,128)} %slice.70.refs_2_, f32[64,512]{1,0:T(8,128)} %copy-done.11, f32[64,512]{1,0:T(8,128)} %get-tuple-element.45.refs_4_, f32[64,512]{1,0:T(8,128)} %get-tuple-element.43.refs_5_, ...), custom_call_target="tpu_custom_call" | custom-call | tf_op jit(solution)/shard_map/slice/pallas_call | solution.py:190
  61.6 0.7 collective-permute-start.14
  62.3 0.9 collective-permute-done.13.refs_1_
  63.1 3.2 %collective-permute-done.14.refs_3_ = f32[64,512]{1,0:T(8,128)S(1)} collective-permute-done((f32[64,512]{1,0:T(8,128)}, f32[64,512]{1,0:T(8,128)S(1)}, u32[]{:S(2)}, u32[]{:S(2)}) %collective-permute-start.14) | collective-permute-done | bytes 131104 | tf_op jit(solution)/shard_map/ppermute | solution.py:196
  66.3 0.7 copy-done.17
  67.0 2.6 %slice.72.refs_2_ = f32[64,512]{1,0:T(8,128)} custom-call(s32[1]{0:T(128)} %bitcast.2.refs_0_, f32[64,512]{1,0:T(8,128)} %copy-done.16, f32[64,512]{1,0:T(8,128)} %get-tuple-element.25.refs_2_, f32[64,512]{1,0:T(8,128)} %copy-done.17, f32[64,512]{1,0:T(8,128)} %get-tuple-element.44.refs_4_, f32[64,512]{1,0:T(8,128)} %get-tuple-element.42.refs_5_, ...), custom_call_target="tpu_custom_call" | custom-call | tf_op jit(solution)/shard_map/slice/pallas_call | solution.py:190
  70.3 0.9 collective-permute-done.15.refs_1_
  71.2 3.4 %collective-permute-done.16.refs_3_ = f32[64,512]{1,0:T(8,128)S(1)} collective-permute-done((f32[64,512]{1,0:T(8,128)}, f32[64,512]{1,0:T(8,128)S(1)}, u32[]{:S(2)}, u32[]{:S(2)}) %collective-permute-start.16) | collective-permute-done | bytes 131104 | tf_op jit(solution)/shard_map/ppermute | solution.py:196
  74.6 0.7 copy-done.15
  75.3 2.7 %slice.73 = (f32[64,512]{1,0:T(8,128)}, f32[64,512]{1,0:T(8,128)}) custom-call(s32[1]{0:T(128)} %bitcast.1.refs_0_, f32[64,512]{1,0:T(8,128)} %copy-done.14, f32[64,512]{1,0:T(8,128)} %slice.72.refs_2_, f32[64,512]{1,0:T(8,128)} %copy-done.15, f32[64,512]{1,0:T(8,128)} %get-tuple-element.45.refs_4_, f32[64,512]{1,0:T(8,128)} %get-tuple-element.43.refs_5_, ...), custom_call_target="tpu_custom_call" | custom-call | tf_op jit(solution)/shard_map/slice/pallas_call | solution.py:190
  78.0 5.8 %collective-permute-start.18 = (f32[64,512]{1,0:T(8,128)}, f32[64,512]{1,0:T(8,128)S(1)}, u32[]{:S(2)}, u32[]{:S(2)}) collective-permute-start(f32[64,512]{1,0:T(8,128)} %get-tuple-element.26.refs_2_), channel_id=1, source_target_pairs={{0,96},{64,1},{1,64},{65,2},{2,65},{66,3},{3,66},{67,11},{11,67},{... | collective-permute-start | bytes 393224 | tf_op jit(solution)/shard_map/ppermute | solution.py:196
  83.8 2.9 %collective-permute-done.18.refs_3_ = f32[64,512]{1,0:T(8,128)S(1)} collective-permute-done((f32[64,512]{1,0:T(8,128)}, f32[64,512]{1,0:T(8,128)S(1)}, u32[]{:S(2)}, u32[]{:S(2)}) %collective-permute-start.18) | collective-permute-done | bytes 131104 | tf_op jit(solution)/shard_map/ppermute | solution.py:196
  87.3 2.7 %slice.74.refs_2_ = f32[64,512]{1,0:T(8,128)} custom-call(s32[1]{0:T(128)} %bitcast.1.refs_0_, f32[64,512]{1,0:T(8,128)} %copy-done.18, f32[64,512]{1,0:T(8,128)} %get-tuple-element.26.refs_2_, f32[64,512]{1,0:T(8,128)} %copy-done.19, f32[64,512]{1,0:T(8,128)} %get-tuple-element.44.refs_4_, f32[64,512]{1,0:T(8,128)} %get-tuple-element.42.refs_5_, ...), custom_call_target="tpu_custom_call" | custom-call | tf_op jit(solution)/shard_map/slice/pallas_call | solution.py:190
  90.0 1.9 %collective-permute-start.20 = (f32[64,512]{1,0:T(8,128)}, f32[64,512]{1,0:T(8,128)S(1)}, u32[]{:S(2)}, u32[]{:S(2)}) collective-permute-start(f32[64,512]{1,0:T(8,128)} %slice.74.refs_2_), channel_id=1, source_target_pairs={{0,96},{64,1},{1,64},{65,2},{2,65},{66,3},{3,66},{67,11},{11,67},{... | collective-permute-start | bytes 393224 | tf_op jit(solution)/shard_map/ppermute | solution.py:196
  91.9 2.9 %collective-permute-done.20.refs_3_ = f32[64,512]{1,0:T(8,128)S(1)} collective-permute-done((f32[64,512]{1,0:T(8,128)}, f32[64,512]{1,0:T(8,128)S(1)}, u32[]{:S(2)}, u32[]{:S(2)}) %collective-permute-start.20) | collective-permute-done | bytes 131104 | tf_op jit(solution)/shard_map/ppermute | solution.py:196
  95.4 2.7 %slice.75 = (f32[64,512]{1,0:T(8,128)}, f32[64,512]{1,0:T(8,128)}) custom-call(s32[1]{0:T(128)} %bitcast.refs_0_, f32[64,512]{1,0:T(8,128)} %copy-done.12, f32[64,512]{1,0:T(8,128)} %slice.74.refs_2_, f32[64,512]{1,0:T(8,128)} %copy-done.13, f32[64,512]{1,0:T(8,128)} %get-tuple-element.45.refs_4_, f32[64,512]{1,0:T(8,128)} %get-tuple-element.43.refs_5_, ...), custom_call_target="tpu_custom_call" | custom-call | tf_op jit(solution)/shard_map/slice/pallas_call | solution.py:190
  98.4 1.7 %collective-permute-start.22 = (f32[64,512]{1,0:T(8,128)}, f32[64,512]{1,0:T(8,128)S(1)}, u32[]{:S(2)}, u32[]{:S(2)}) collective-permute-start(f32[64,512]{1,0:T(8,128)} %get-tuple-element.27.refs_2_), channel_id=1, source_target_pairs={{0,96},{64,1},{1,64},{65,2},{2,65},{66,3},{3,66},{67,11},{11,67},{... | collective-permute-start | bytes 393224 | tf_op jit(solution)/shard_map/ppermute | solution.py:196
  100.2 3.1 %collective-permute-done.22.refs_3_ = f32[64,512]{1,0:T(8,128)S(1)} collective-permute-done((f32[64,512]{1,0:T(8,128)}, f32[64,512]{1,0:T(8,128)S(1)}, u32[]{:S(2)}, u32[]{:S(2)}) %collective-permute-start.22) | collective-permute-done | bytes 131104 | tf_op jit(solution)/shard_map/ppermute | solution.py:196
  103.9 2.7 %slice.76.own = f32[64,512]{1,0:T(8,128)} custom-call(s32[1]{0:T(128)} %bitcast.refs_0_, f32[64,512]{1,0:T(8,128)} %copy-done.8, f32[64,512]{1,0:T(8,128)} %get-tuple-element.27.refs_2_, f32[64,512]{1,0:T(8,128)} %copy-done.9, f32[64,512]{1,0:T(8,128)} %get-tuple-element.44.refs_4_, f32[64,512]{1,0:T(8,128)} %get-tuple-element.42.refs_5_, ...), custom_call_target="tpu_custom_call" | custom-call | tf_op jit(solution)/shard_map/slice/pallas_call | solution.py:190
  107.2 1.1 collective-permute-start.24
  108.4 2.9 %collective-permute-start.26 = (f32[64,512]{1,0:T(8,128)S(1)}, f32[64,512]{1,0:T(8,128)S(1)}, u32[]{:S(2)}, u32[]{:S(2)}) collective-permute-start(f32[64,512]{1,0:T(8,128)S(1)} %get-tuple-element.39), channel_id=1, source_target_pairs={{0,128},{64,129},{1,130},{65,131},{2,132},{66,133},{3,134},{67,135... | collective-permute-start | bytes 393224 | tf_op jit(solution)/shard_map/ppermute | solution.py:196
  111.3 16.1 %collective-permute-start.27 = (f32[64,512]{1,0:T(8,128)S(1)}, f32[64,512]{1,0:T(8,128)S(1)}, u32[]{:S(2)}, u32[]{:S(2)}) collective-permute-start(f32[64,512]{1,0:T(8,128)S(1)} %get-tuple-element.38), channel_id=1, source_target_pairs={{0,64},{64,65},{1,66},{65,67},{2,68},{66,69},{3,70},{67,71},{11,72... | collective-permute-start | bytes 393224 | tf_op jit(solution)/shard_map/ppermute | solution.py:196
  127.4 1.3 collective-permute-start.28
  130.0 2.0 %leave.1 = f32[64,512]{1,0:T(8,128)} custom-call(f32[64,512]{1,0:T(8,128)} %copy-done.23, f32[64,512]{1,0:T(8,128)} %slice.76.own, f32[64,512]{1,0:T(8,128)} %copy-done.24, bf16[64,192]{1,0:T(8,128)(2,1)} %get-tuple-element.47.refs_7_.rhi, bf16[64,192]{1,0:T(8,128)(2,1)} %get-tuple-element.46.refs_8_.rlo), custom_call_target="tpu_custom_call" | custom-call | tf_op jit(solution)/shard_map/leave/pallas_call | solution.py:190
  132.0 1.3 collective-permute-start.25
  133.2 1.3 collective-permute-start.29
  134.6 1.9 %collective-permute-start.30 = (f32[64,512]{1,0:T(8,128)}, f32[64,512]{1,0:T(8,128)S(1)}, u32[]{:S(2)}, u32[]{:S(2)}) collective-permute-start(f32[64,512]{1,0:T(8,128)} %leave.1), channel_id=1, source_target_pairs={{128,192},{192,193},{129,194},{193,195},{130,196},{194,197},{131,1... | collective-permute-start | bytes 393224 | tf_op jit(solution)/shard_map/ppermute | solution.py:196
  136.6 5.6 %collective-permute-done.25 = f32[64,512]{1,0:T(8,128)S(1)} collective-permute-done((f32[64,512]{1,0:T(8,128)}, f32[64,512]{1,0:T(8,128)S(1)}, u32[]{:S(2)}, u32[]{:S(2)}) %collective-permute-start.25) | collective-permute-done | bytes 131104 | tf_op jit(solution)/shard_map/ppermute | solution.py:196
  142.2 7.9 %collective-permute-done.29 = f32[64,512]{1,0:T(8,128)S(1)} collective-permute-done((f32[64,512]{1,0:T(8,128)}, f32[64,512]{1,0:T(8,128)S(1)}, u32[]{:S(2)}, u32[]{:S(2)}) %collective-permute-start.29) | collective-permute-done | bytes 131104 | tf_op jit(solution)/shard_map/ppermute | solution.py:196
  150.1 0.8 maximum_bitcast_fusion
  (96 shorter events, 9.7 us)
Async XLA Ops:
  4.0 5.3 %collective-permute-start = (f32[64,512]{1,0:T(8,128)}, f32[64,512]{1,0:T(8,128)S(1)}, u32[]{:S(2)}, u32[]{:S(2)}) collective-permute-start(f32[64,512]{1,0:T(8,128)} %get-tuple-element.18), channel_id=1, source_target_pairs={{0,0},{1,64},{2,1},{3,65},{4,2},{5,66},{6,3},{7,67},{8,11},{9,75},... | collective-permute-start | bytes 393224 | tf_op jit(solution)/shard_map/ppermute | solution.py:196
  4.6 23.9 %collective-permute-start.1 = (f32[64,512]{1,0:T(8,128)}, f32[64,512]{1,0:T(8,128)S(1)}, u32[]{:S(2)}, u32[]{:S(2)}) collective-permute-start(f32[64,512]{1,0:T(8,128)} %get-tuple-element.19), channel_id=1, source_target_pairs={{0,4},{1,68},{2,5},{3,69},{4,6},{5,70},{6,7},{7,71},{8,15},{9,79},... | collective-permute-start | bytes 393224 | tf_op jit(solution)/shard_map/ppermute | solution.py:196
  5.3 24.5 %collective-permute-start.2 = (f32[64,512]{1,0:T(8,128)}, f32[64,512]{1,0:T(8,128)S(1)}, u32[]{:S(2)}, u32[]{:S(2)}) collective-permute-start(f32[64,512]{1,0:T(8,128)} %get-tuple-element.20), channel_id=1, source_target_pairs={{0,128},{1,192},{2,129},{3,193},{4,130},{5,194},{6,131},{7,195},{8... | collective-permute-start | bytes 393224 | tf_op jit(solution)/shard_map/ppermute | solution.py:196
  6.6 30.8 %collective-permute-start.5 = (f32[64,512]{1,0:T(8,128)}, f32[64,512]{1,0:T(8,128)S(1)}, u32[]{:S(2)}, u32[]{:S(2)}) collective-permute-start(f32[64,512]{1,0:T(8,128)} %get-tuple-element.21), channel_id=1, source_target_pairs={{0,0},{1,64},{2,1},{3,65},{4,2},{5,66},{6,3},{7,67},{8,11},{9,75},... | collective-permute-start | bytes 393224 | tf_op jit(solution)/shard_map/ppermute | solution.py:196
  7.3 30.2 %collective-permute-start.6 = (f32[64,512]{1,0:T(8,128)}, f32[64,512]{1,0:T(8,128)S(1)}, u32[]{:S(2)}, u32[]{:S(2)}) collective-permute-start(f32[64,512]{1,0:T(8,128)} %get-tuple-element.22), channel_id=1, source_target_pairs={{0,4},{1,68},{2,5},{3,69},{4,6},{5,70},{6,7},{7,71},{8,15},{9,79},... | collective-permute-start | bytes 393224 | tf_op jit(solution)/shard_map/ppermute | solution.py:196
  9.1 19.4 %copy-start.29 = (f32[64,512]{1,0:T(8,128)S(1)}, f32[64,512]{1,0:T(8,128)}, u32[]{:S(2)}) copy-start(f32[64,512]{1,0:T(8,128)} %get-tuple-element.23) | copy-start | bytes 393220
  9.2 25.9 %copy-start.2 = (f32[64,512]{1,0:T(8,128)}, f32[64,512]{1,0:T(8,128)S(1)}, u32[]{:S(2)}) copy-start(f32[64,512]{1,0:T(8,128)S(1)} %collective-permute-done.a) | copy-start | bytes 393220
  9.3 44.6 %collective-permute-start.12 = (f32[2,64,512]{2,1,0:T(8,128)S(1)}, f32[2,64,512]{2,1,0:T(8,128)S(1)}, u32[]{:S(2)}, u32[]{:S(2)}) collective-permute-start(f32[2,64,512]{2,1,0:T(8,128)S(1)} %get-tuple-element.31), channel_id=1, source_target_pairs={{192,0},{193,64},{194,1},{195,65},{196,2},{197,66},{198,3},{199,67... | collective-permute-start | bytes 786440 | tf_op jit(solution)/shard_map/ppermute | solution.py:196
  28.5 6.6 %copy-start.3 = (f32[64,512]{1,0:T(8,128)}, f32[64,512]{1,0:T(8,128)S(1)}, u32[]{:S(2)}) copy-start(f32[64,512]{1,0:T(8,128)S(1)} %collective-permute-done.1.b) | copy-start | bytes 393220
  28.6 17.1 %collective-permute-start.7 = (f32[64,512]{1,0:T(8,128)S(1)}, f32[64,512]{1,0:T(8,128)S(1)}, u32[]{:S(2)}, u32[]{:S(2)}) collective-permute-start(f32[64,512]{1,0:T(8,128)S(1)} %copy-done.29), channel_id=1, source_target_pairs={{0,128},{1,192},{2,129},{3,193},{4,130},{5,194},{6,131},{7,195},{8... | collective-permute-start | bytes 393224 | tf_op jit(solution)/shard_map/ppermute | solution.py:196
  29.9 5.3 %copy-start.4 = (f32[64,512]{1,0:T(8,128)}, f32[64,512]{1,0:T(8,128)S(1)}, u32[]{:S(2)}) copy-start(f32[64,512]{1,0:T(8,128)S(1)} %collective-permute-done.2.c) | copy-start | bytes 393220
  29.9 8.1 %copy-start.25 = (bf16[64,192]{1,0:T(8,128)(2,1)S(1)}, bf16[64,192]{1,0:T(8,128)(2,1)}, u32[]{:S(2)}) copy-start(bf16[64,192]{1,0:T(8,128)(2,1)} %constant.153) | copy-start | bytes 73732
  29.9 8.1 %copy-start.26 = (bf16[64,192]{1,0:T(8,128)(2,1)S(1)}, bf16[64,192]{1,0:T(8,128)(2,1)}, u32[]{:S(2)}) copy-start(bf16[64,192]{1,0:T(8,128)(2,1)} %constant.154) | copy-start | bytes 73732
  29.9 8.1 %copy-start.27 = (bf16[64,192]{1,0:T(8,128)(2,1)S(1)}, bf16[64,192]{1,0:T(8,128)(2,1)}, u32[]{:S(2)}) copy-start(bf16[64,192]{1,0:T(8,128)(2,1)} %constant.157) | copy-start | bytes 73732
  29.9 8.1 %copy-start.28 = (bf16[64,192]{1,0:T(8,128)(2,1)S(1)}, bf16[64,192]{1,0:T(8,128)(2,1)}, u32[]{:S(2)}) copy-start(bf16[64,192]{1,0:T(8,128)(2,1)} %constant.160) | copy-start | bytes 73732
  29.9 24.6 %collective-permute-start.11 = (f32[2,64,512]{2,1,0:T(8,128)S(1)}, f32[2,64,512]{2,1,0:T(8,128)S(1)}, u32[]{:S(2)}, u32[]{:S(2)}) collective-permute-start(f32[2,64,512]{2,1,0:T(8,128)S(1)} %get-tuple-element.32), channel_id=1, source_target_pairs={{128,0},{129,64},{130,1},{131,65},{132,2},{133,66},{134,3},{135,67... | collective-permute-start | bytes 786440 | tf_op jit(solution)/shard_map/ppermute | solution.py:196
  37.5 10.2 %collective-permute-start.3 = (f32[64,512]{1,0:T(8,128)}, f32[64,512]{1,0:T(8,128)S(1)}, u32[]{:S(2)}, u32[]{:S(2)}) collective-permute-start(f32[64,512]{1,0:T(8,128)} %enter.1.refs_2_), channel_id=1, source_target_pairs={{0,64},{64,0},{1,65},{65,1},{2,66},{66,2},{3,67},{67,3},{11,75},{7... | collective-permute-start | bytes 393224 | tf_op jit(solution)/shard_map/ppermute | solution.py:196
  37.5 10.1 %collective-permute-start.4 = (f32[64,512]{1,0:T(8,128)}, f32[64,512]{1,0:T(8,128)S(1)}, u32[]{:S(2)}, u32[]{:S(2)}) collective-permute-start(f32[64,512]{1,0:T(8,128)} %enter.1.refs_2_), channel_id=1, source_target_pairs={{0,96},{64,1},{1,64},{65,2},{2,65},{66,3},{3,66},{67,11},{11,67},{... | collective-permute-start | bytes 393224 | tf_op jit(solution)/shard_map/ppermute | solution.py:196
  45.7 2.0 %copy-start.5 = (f32[64,512]{1,0:T(8,128)}, f32[64,512]{1,0:T(8,128)S(1)}, u32[]{:S(2)}) copy-start(f32[64,512]{1,0:T(8,128)S(1)} %collective-permute-done.7.refs_6_) | copy-start | bytes 393220
  45.7 11.8 %collective-permute-start.10 = (f32[2,64,512]{2,1,0:T(8,128)S(1)}, f32[2,64,512]{2,1,0:T(8,128)S(1)}, u32[]{:S(2)}, u32[]{:S(2)}) collective-permute-start(f32[2,64,512]{2,1,0:T(8,128)S(1)} %get-tuple-element.33), channel_id=1, source_target_pairs={{64,0},{65,64},{66,1},{67,65},{68,2},{69,66},{70,3},{71,67},{72,11... | collective-permute-start | bytes 786440 | tf_op jit(solution)/shard_map/ppermute | solution.py:196
  51.0 7.3 %collective-permute-start.8 = (f32[64,512]{1,0:T(8,128)}, f32[64,512]{1,0:T(8,128)S(1)}, u32[]{:S(2)}, u32[]{:S(2)}) collective-permute-start(f32[64,512]{1,0:T(8,128)} %slice.70.refs_2_), channel_id=1, source_target_pairs={{0,64},{64,0},{1,65},{65,1},{2,66},{66,2},{3,67},{67,3},{11,75},{7... | collective-permute-start | bytes 393224 | tf_op jit(solution)/shard_map/ppermute | solution.py:196
  51.0 7.3 %collective-permute-start.9 = (f32[64,512]{1,0:T(8,128)}, f32[64,512]{1,0:T(8,128)S(1)}, u32[]{:S(2)}, u32[]{:S(2)}) collective-permute-start(f32[64,512]{1,0:T(8,128)} %slice.70.refs_2_), channel_id=1, source_target_pairs={{0,96},{64,1},{1,64},{65,2},{2,65},{66,3},{3,66},{67,11},{11,67},{... | collective-permute-start | bytes 393224 | tf_op jit(solution)/shard_map/ppermute | solution.py:196
  61.6 1.6 %collective-permute-start.13 = (f32[64,512]{1,0:T(8,128)}, f32[64,512]{1,0:T(8,128)S(1)}, u32[]{:S(2)}, u32[]{:S(2)}) collective-permute-start(f32[64,512]{1,0:T(8,128)} %get-tuple-element.25.refs_2_), channel_id=1, source_target_pairs={{0,64},{64,0},{1,65},{65,1},{2,66},{66,2},{3,67},{67,3},{11,75},{7... | collective-permute-start | bytes 393224 | tf_op jit(solution)/shard_map/ppermute | solution.py:196
  61.6 4.7 %collective-permute-start.14 = (f32[64,512]{1,0:T(8,128)}, f32[64,512]{1,0:T(8,128)S(1)}, u32[]{:S(2)}, u32[]{:S(2)}) collective-permute-start(f32[64,512]{1,0:T(8,128)} %get-tuple-element.25.refs_2_), channel_id=1, source_target_pairs={{0,96},{64,1},{1,64},{65,2},{2,65},{66,3},{3,66},{67,11},{11,67},{... | collective-permute-start | bytes 393224 | tf_op jit(solution)/shard_map/ppermute | solution.py:196
  63.1 3.2 %copy-start.16 = (f32[64,512]{1,0:T(8,128)}, f32[64,512]{1,0:T(8,128)S(1)}, u32[]{:S(2)}) copy-start(f32[64,512]{1,0:T(8,128)S(1)} %collective-permute-done.13.refs_1_) | copy-start | bytes 393220
  69.6 1.6 %collective-permute-start.15 = (f32[64,512]{1,0:T(8,128)}, f32[64,512]{1,0:T(8,128)S(1)}, u32[]{:S(2)}, u32[]{:S(2)}) collective-permute-start(f32[64,512]{1,0:T(8,128)} %slice.72.refs_2_), channel_id=1, source_target_pairs={{0,64},{64,0},{1,65},{65,1},{2,66},{66,2},{3,67},{67,3},{11,75},{7... | collective-permute-start | bytes 393224 | tf_op jit(solution)/shard_map/ppermute | solution.py:196
  70.0 4.6 %collective-permute-start.16 = (f32[64,512]{1,0:T(8,128)}, f32[64,512]{1,0:T(8,128)S(1)}, u32[]{:S(2)}, u32[]{:S(2)}) collective-permute-start(f32[64,512]{1,0:T(8,128)} %slice.72.refs_2_), channel_id=1, source_target_pairs={{0,96},{64,1},{1,64},{65,2},{2,65},{66,3},{3,66},{67,11},{11,67},{... | collective-permute-start | bytes 393224 | tf_op jit(solution)/shard_map/ppermute | solution.py:196
  71.2 3.4 %copy-start.14 = (f32[64,512]{1,0:T(8,128)}, f32[64,512]{1,0:T(8,128)S(1)}, u32[]{:S(2)}) copy-start(f32[64,512]{1,0:T(8,128)S(1)} %collective-permute-done.15.refs_1_) | copy-start | bytes 393220
  77.9 5.9 %collective-permute-start.17 = (f32[64,512]{1,0:T(8,128)}, f32[64,512]{1,0:T(8,128)S(1)}, u32[]{:S(2)}, u32[]{:S(2)}) collective-permute-start(f32[64,512]{1,0:T(8,128)} %get-tuple-element.26.refs_2_), channel_id=1, source_target_pairs={{0,64},{64,0},{1,65},{65,1},{2,66},{66,2},{3,67},{67,3},{11,75},{7... | collective-permute-start | bytes 393224 | tf_op jit(solution)/shard_map/ppermute | solution.py:196
  78.0 8.6 %collective-permute-start.18 = (f32[64,512]{1,0:T(8,128)}, f32[64,512]{1,0:T(8,128)S(1)}, u32[]{:S(2)}, u32[]{:S(2)}) collective-permute-start(f32[64,512]{1,0:T(8,128)} %get-tuple-element.26.refs_2_), channel_id=1, source_target_pairs={{0,96},{64,1},{1,64},{65,2},{2,65},{66,3},{3,66},{67,11},{11,67},{... | collective-permute-start | bytes 393224 | tf_op jit(solution)/shard_map/ppermute | solution.py:196
  83.8 2.9 %copy-start.18 = (f32[64,512]{1,0:T(8,128)}, f32[64,512]{1,0:T(8,128)S(1)}, u32[]{:S(2)}) copy-start(f32[64,512]{1,0:T(8,128)S(1)} %collective-permute-done.17.refs_1_) | copy-start | bytes 393220
  90.0 1.9 %collective-permute-start.19 = (f32[64,512]{1,0:T(8,128)}, f32[64,512]{1,0:T(8,128)S(1)}, u32[]{:S(2)}, u32[]{:S(2)}) collective-permute-start(f32[64,512]{1,0:T(8,128)} %slice.74.refs_2_), channel_id=1, source_target_pairs={{0,64},{64,0},{1,65},{65,1},{2,66},{66,2},{3,67},{67,3},{11,75},{7... | collective-permute-start | bytes 393224 | tf_op jit(solution)/shard_map/ppermute | solution.py:196
  90.0 4.8 %collective-permute-start.20 = (f32[64,512]{1,0:T(8,128)}, f32[64,512]{1,0:T(8,128)S(1)}, u32[]{:S(2)}, u32[]{:S(2)}) collective-permute-start(f32[64,512]{1,0:T(8,128)} %slice.74.refs_2_), channel_id=1, source_target_pairs={{0,96},{64,1},{1,64},{65,2},{2,65},{66,3},{3,66},{67,11},{11,67},{... | collective-permute-start | bytes 393224 | tf_op jit(solution)/shard_map/ppermute | solution.py:196
  91.9 2.9 %copy-start.12 = (f32[64,512]{1,0:T(8,128)}, f32[64,512]{1,0:T(8,128)S(1)}, u32[]{:S(2)}) copy-start(f32[64,512]{1,0:T(8,128)S(1)} %collective-permute-done.19.refs_1_) | copy-start | bytes 393220
  98.0 2.1 %collective-permute-start.21 = (f32[64,512]{1,0:T(8,128)}, f32[64,512]{1,0:T(8,128)S(1)}, u32[]{:S(2)}, u32[]{:S(2)}) collective-permute-start(f32[64,512]{1,0:T(8,128)} %get-tuple-element.27.refs_2_), channel_id=1, source_target_pairs={{0,64},{64,0},{1,65},{65,1},{2,66},{66,2},{3,67},{67,3},{11,75},{7... | collective-permute-start | bytes 393224 | tf_op jit(solution)/shard_map/ppermute | solution.py:196
  98.4 4.9 %collective-permute-start.22 = (f32[64,512]{1,0:T(8,128)}, f32[64,512]{1,0:T(8,128)S(1)}, u32[]{:S(2)}, u32[]{:S(2)}) collective-permute-start(f32[64,512]{1,0:T(8,128)} %get-tuple-element.27.refs_2_), channel_id=1, source_target_pairs={{0,96},{64,1},{1,64},{65,2},{2,65},{66,3},{3,66},{67,11},{11,67},{... | collective-permute-start | bytes 393224 | tf_op jit(solution)/shard_map/ppermute | solution.py:196
  100.1 8.2 %copy-start.20 = (f32[64,512]{1,0:T(8,128)S(1)}, f32[64,512]{1,0:T(8,128)}, u32[]{:S(2)}) copy-start(f32[64,512]{1,0:T(8,128)} %get-tuple-element.30) | copy-start | bytes 393220
  100.1 8.2 %copy-start.21 = (f32[64,512]{1,0:T(8,128)S(1)}, f32[64,512]{1,0:T(8,128)}, u32[]{:S(2)}) copy-start(f32[64,512]{1,0:T(8,128)} %get-tuple-element.29) | copy-start | bytes 393220
  100.1 8.2 %copy-start.22 = (f32[64,512]{1,0:T(8,128)S(1)}, f32[64,512]{1,0:T(8,128)}, u32[]{:S(2)}) copy-start(f32[64,512]{1,0:T(8,128)} %get-tuple-element.28) | copy-start | bytes 393220
  100.1 3.1 %copy-start.8 = (f32[64,512]{1,0:T(8,128)}, f32[64,512]{1,0:T(8,128)S(1)}, u32[]{:S(2)}) copy-start(f32[64,512]{1,0:T(8,128)S(1)} %collective-permute-done.21.refs_1_) | copy-start | bytes 393220
  106.6 22.1 %collective-permute-start.23 = (f32[64,512]{1,0:T(8,128)}, f32[64,512]{1,0:T(8,128)S(1)}, u32[]{:S(2)}, u32[]{:S(2)}) collective-permute-start(f32[64,512]{1,0:T(8,128)} %slice.76.own), channel_id=1, source_target_pairs={{0,64},{64,0},{1,65},{65,1},{2,66},{66,2},{3,67},{67,3},{11,75},{7... | collective-permute-start | bytes 393224 | tf_op jit(solution)/shard_map/ppermute | solution.py:196
  107.2 21.5 %collective-permute-start.24 = (f32[64,512]{1,0:T(8,128)}, f32[64,512]{1,0:T(8,128)S(1)}, u32[]{:S(2)}, u32[]{:S(2)}) collective-permute-start(f32[64,512]{1,0:T(8,128)} %slice.76.own), channel_id=1, source_target_pairs={{0,96},{64,1},{1,64},{65,2},{2,65},{66,3},{3,66},{67,11},{11,67},{... | collective-permute-start | bytes 393224 | tf_op jit(solution)/shard_map/ppermute | solution.py:196
  108.4 26.2 %collective-permute-start.26 = (f32[64,512]{1,0:T(8,128)S(1)}, f32[64,512]{1,0:T(8,128)S(1)}, u32[]{:S(2)}, u32[]{:S(2)}) collective-permute-start(f32[64,512]{1,0:T(8,128)S(1)} %get-tuple-element.39), channel_id=1, source_target_pairs={{0,128},{64,129},{1,130},{65,131},{2,132},{66,133},{3,134},{67,135... | collective-permute-start | bytes 393224 | tf_op jit(solution)/shard_map/ppermute | solution.py:196
  111.3 25.2 %collective-permute-start.27 = (f32[64,512]{1,0:T(8,128)S(1)}, f32[64,512]{1,0:T(8,128)S(1)}, u32[]{:S(2)}, u32[]{:S(2)}) collective-permute-start(f32[64,512]{1,0:T(8,128)S(1)} %get-tuple-element.38), channel_id=1, source_target_pairs={{0,64},{64,65},{1,66},{65,67},{2,68},{66,69},{3,70},{67,71},{11,72... | collective-permute-start | bytes 393224 | tf_op jit(solution)/shard_map/ppermute | solution.py:196
  127.4 9.2 %collective-permute-start.28 = (f32[64,512]{1,0:T(8,128)S(1)}, f32[64,512]{1,0:T(8,128)S(1)}, u32[]{:S(2)}, u32[]{:S(2)}) collective-permute-start(f32[64,512]{1,0:T(8,128)S(1)} %get-tuple-element.37), channel_id=1, source_target_pairs={{0,0},{64,1},{1,2},{65,3},{2,4},{66,5},{3,6},{67,7},{11,8},{75,9},... | collective-permute-start | bytes 393224 | tf_op jit(solution)/shard_map/ppermute | solution.py:196
  132.0 10.2 %collective-permute-start.25 = (f32[64,512]{1,0:T(8,128)}, f32[64,512]{1,0:T(8,128)S(1)}, u32[]{:S(2)}, u32[]{:S(2)}) collective-permute-start(f32[64,512]{1,0:T(8,128)} %leave.1), channel_id=1, source_target_pairs={{0,192},{64,193},{1,194},{65,195},{2,196},{66,197},{3,198},{67,199... | collective-permute-start | bytes 393224 | tf_op jit(solution)/shard_map/ppermute | solution.py:196
  133.2 16.8 %collective-permute-start.29 = (f32[64,512]{1,0:T(8,128)}, f32[64,512]{1,0:T(8,128)S(1)}, u32[]{:S(2)}, u32[]{:S(2)}) collective-permute-start(f32[64,512]{1,0:T(8,128)} %leave.1), channel_id=1, source_target_pairs={{4,192},{68,193},{5,194},{69,195},{6,196},{70,197},{7,198},{71,199... | collective-permute-start | bytes 393224 | tf_op jit(solution)/shard_map/ppermute | solution.py:196
  134.6 15.5 %collective-permute-start.30 = (f32[64,512]{1,0:T(8,128)}, f32[64,512]{1,0:T(8,128)S(1)}, u32[]{:S(2)}, u32[]{:S(2)}) collective-permute-start(f32[64,512]{1,0:T(8,128)} %leave.1), channel_id=1, source_target_pairs={{128,192},{192,193},{129,194},{193,195},{130,196},{194,197},{131,1... | collective-permute-start | bytes 393224 | tf_op jit(solution)/shard_map/ppermute | solution.py:196
  (14 other events, 10.3 us)

commit v2 on v1

--- a/solution.py
+++ b/solution.py
@@ -1,3 +1,5 @@
+import functools
+
 import jax
 import jax.numpy as jnp
 import numpy as np
@@ -14,7 +16,6 @@
 SLABS = 4
 TILES = 64
 AXES = ("depth", "tile")
-USE_KERNELS = True
 
 
 def device_at(x, y, z, core):
@@ -22,12 +23,11 @@
 
 
 def worker(slot, tile):
-    chip, core = divmod(tile, 2)
-    x_lo, rest = divmod(chip, 16)
-    y, z = divmod(rest, 4)
-    z = z if y % 2 == 0 else 3 - z
+    x_lo, rest = divmod(tile, 32)
+    y, z = divmod(rest, 8)
     y = y if x_lo == 0 else 3 - y
-    return device_at(2 * (slot // 2) + x_lo, y, z + 4 * (slot % 2), core)
+    core = 0 if z // 4 == slot % 2 else 1
+    return device_at(2 * (slot // 2) + x_lo, y, z if core == 0 else 7 - z, core)
 
 
 def home(depth, tile):
@@ -36,7 +36,7 @@
 
 INNER = [(worker(k, p), worker(k, p ^ 1)) for k in range(4) for p in range(TILES)]
 OUTER = [
-    (worker(k, p), worker(k, (p + 1) % TILES if p % 2 else (p - 1) % TILES))
+    (worker(k, p), worker(k, (p + 1 if p % 2 else p - 1) % TILES))
     for k in range(4)
     for p in range(TILES)
 ]
@@ -146,32 +146,33 @@
     return out
 
 
-def prepare_kernel(order, incident, delta, beta, *outs):
-    depth = order[3]
-    for slot in range(VIEWS):
-        view = order[slot]
-        even = transmission(delta[view, 0], beta[view, 0])
-        odd = transmission(delta[view, 1], beta[view, 1])
-        entering = jnp.concatenate([incident[0, view], incident[1, view]], axis=0)
-        outs[slot][...] = times(even, entering)
-        outs[VIEWS + slot][...] = odd
-        place = lax.rem(depth + 5 - slot, 3)
-        outs[2 * VIEWS][place, 0] = even
-        outs[2 * VIEWS][place, 1] = odd
+def prepare_kernel(order, depth, incident, delta, beta, *outs):
+    @pl.when(depth[0] == 0)
+    def _():
+        for slot in range(VIEWS):
+            view = order[slot]
+            entering = jnp.concatenate([incident[0, view], incident[1, view]], axis=0)
+            outs[slot][...] = times(transmission(delta[view, 0], beta[view, 0]), entering)
+            outs[VIEWS + slot][...] = transmission(delta[view, 1], beta[view, 1])
+
+    @pl.when(depth[0] > 0)
+    def _():
+        for m in range(VIEWS):
+            view = order[lax.rem(depth[0] + 5 - m, 3)]
+            for half in range(2):
+                outs[2 * VIEWS + m][half] = transmission(delta[view, half], beta[view, half])
 
 
 def first_kernel(a, b, c, chi, clo, out):
     out[...] = column_blur(a[...] + b[...] + c[...], chi[...], clo[...])
 
 
-def middle_kernel(slab_end, n_trans, which, inner, own, outer, *refs):
-    trans = refs[:n_trans]
-    rhi, rlo, chi, clo = refs[n_trans : n_trans + 4]
-    outs = refs[n_trans + 4 :]
+def middle_kernel(slab_end, half, which, inner, own, outer, *refs):
+    trans, (rhi, rlo, chi, clo), outs = refs[:VIEWS], refs[VIEWS : VIEWS + 4], refs[VIEWS + 4 :]
     field = row_blur(inner[...], own[...], outer[...], rhi[...], rlo[...])
     if slab_end:
         outs[1][...] = field
-    t = pick(which[0], [r[...] for r in trans])
+    t = pick(which[0], [r[...] if half is None else r[half] for r in trans])
     outs[0][...] = column_blur(times(t, field), chi[...], clo[...])
 
 
@@ -179,83 +180,88 @@
     out[...] = row_blur(inner[...], own[...], outer[...], rhi[...], rlo[...])
 
 
+def assemble_kernel(depth, *refs):
+    early, late, out = refs[:VIEWS], refs[VIEWS : 2 * VIEWS], refs[2 * VIEWS]
+    for slot in range(VIEWS):
+        value = late[slot][...] + pick(lax.rem(depth[0] + 3 - slot, 3), [r[...] for r in early])
+        out[0, slot, 0] = value[:ROWS]
+        out[1, slot, 0] = value[ROWS:]
+
+
 FIELD = jax.ShapeDtypeStruct((2 * ROWS, COLS), jnp.float32)
-
-
-def call(kernel, out_shape, args, name, scalar_first=False):
-    vmem = pl.BlockSpec(memory_space=pltpu.VMEM)
-    smem = pl.BlockSpec(memory_space=pltpu.SMEM)
-    specs = [smem if scalar_first and i == 0 else vmem for i in range(len(args))]
-    outs = jax.tree.map(lambda _: vmem, out_shape)
+PAIR = jax.ShapeDtypeStruct((2, 2 * ROWS, COLS), jnp.float32)
+
+
+def call(kernel, out_shape, args, scalars=0, hbm=(), out_hbm=False):
+    vmem, smem = pl.BlockSpec(memory_space=pltpu.VMEM), pl.BlockSpec(memory_space=pltpu.SMEM)
+    specs, held = [], []
+    for i, arg in enumerate(args):
+        scalar = i < scalars
+        specs.append(smem if scalar else vmem)
+        held.append(arg if scalar or i in hbm else pltpu.with_memory_space_constraint(arg, pltpu.VMEM))
+    shapes = out_shape if out_hbm else jax.tree.map(lambda s: pltpu.VMEM(s.shape, s.dtype), out_shape)
     return pl.pallas_call(
-        kernel, out_shape=out_shape, in_specs=specs, out_specs=outs, name=name, interpret=not USE_KERNELS
-    )(*args)
+        kernel, out_shape=shapes, in_specs=specs, out_specs=jax.tree.map(lambda _: vmem, out_shape)
+    )(*held)
 
 
 def permute(value, pairs):
     return lax.ppermute(value, AXES, pairs)
 
 
-def per_device(incident, delta, beta, view_order):
+def propagate(incident, delta, beta, view_order):
     depth, tile = lax.axis_index("depth"), lax.axis_index("tile")
-    core = depth % 2
-    slot = (depth // 2) * 2 + (tile % 8) // 4
+    chip_z, x_lo = tile % 8, tile // 32
+    slot = jnp.minimum((depth // 2) * 2 + chip_z // 4, VIEWS - 1)
+    row_z = jnp.where(depth % 2 == 0, chip_z, 7 - chip_z)
+    row_y = jnp.where(x_lo == 0, tile % 32 // 8, 3 - tile % 32 // 8)
+    place = x_lo * 32 + row_y * 8 + row_z
 
     chi, clo = halves(column_matrix())
     even, odd = row_matrix(0), row_matrix(1)
-    edge = jnp.logical_or(
-        jnp.logical_and(core == 0, tile % 32 // 8 + tile // 32 * 4 + tile % 4 == 0),
-        jnp.logical_and(core == 1, jnp.logical_and(tile // 32 == 1, tile % 32 // 8 + tile % 4 == 0)),
-    )
+    edge = jnp.logical_or(place == 0, place == TILES - 1)
     keep = jnp.logical_or(jnp.logical_not(edge), jnp.arange(6 * ROWS)[None, :] < 4 * ROWS)
     (ehi, elo), (ohi, olo) = halves(even), halves(odd)
-    rhi = jnp.where(keep, jnp.where(core == 0, ehi, ohi), 0)
-    rlo = jnp.where(keep, jnp.where(core == 0, elo, olo), 0)
-
-    scalars = jnp.concatenate([view_order, depth[None]])
-    pair = jax.ShapeDtypeStruct((VIEWS, 2) + FIELD.shape, jnp.float32)
+    rhi = jnp.where(keep, jnp.where(place % 2 == 0, ehi, ohi), 0)
+    rlo = jnp.where(keep, jnp.where(place % 2 == 0, elo, olo), 0)
+
     sent = call(
-        prepare_kernel, [FIELD] * (2 * VIEWS) + [pair], (scalars, incident, delta, beta), "prepare", scalar_first=True
+        prepare_kernel,
+        [FIELD] * (2 * VIEWS) + [PAIR] * VIEWS,
+        (view_order, depth[None], incident, delta, beta),
+        scalars=2,
+        hbm=(2, 3, 4),
     )
-    entering, second, rest = sent[:VIEWS], sent[VIEWS : 2 * VIEWS], sent[2 * VIEWS]
+    entering, second, rest = sent[:VIEWS], sent[VIEWS : 2 * VIEWS], sent[2 * VIEWS :]
 
     def from_first(values):
-        return [
-            permute(values[k], [(home(0, p), worker(k, p)) for p in range(TILES)]) for k in range(VIEWS)
-        ]
+        return [permute(values[k], [(home(0, p), worker(k, p)) for p in range(TILES)]) for k in range(VIEWS)]
 
     starts = from_first(entering)
     seconds = from_first(second)
     later = [
-        permute(
-            rest[m],
-            [(home(1 + (m + k) % 3, p), worker(k, p)) for k in range(VIEWS) for p in range(TILES)],
-        )
+        permute(rest[m], [(home(1 + (m + k) % 3, p), worker(k, p)) for k in range(VIEWS) for p in range(TILES)])
         for m in range(3)
     ]
-
-    own = call(first_kernel, FIELD, (*starts, chi, clo), "enter")
+    own = call(first_kernel, FIELD, (*starts, chi, clo))
     slabs = []
     for piece in range(2 * SLABS):
         inner = permute(own, INNER)
         outer = permute(own, OUTER)
         if piece == 2 * SLABS - 1:
-            slabs.append(call(last_kernel, FIELD, (inner, own, outer, rhi, rlo), "leave"))
+            slabs.append(call(last_kernel, FIELD, (inner, own, outer, rhi, rlo)))
             break
+        slab_end = piece % 2 == 1
         nxt = piece + 1
         if nxt == 1:
-            trans = list(seconds)
-            which = jnp.minimum(slot, 2)[None]
+            t, half, which = seconds, None, slot
         else:
-            trans = [v[nxt % 2] for v in later]
-            which = ((nxt // 2 + 5 - jnp.minimum(slot, 2)) % 3)[None]
-        slab_end = piece % 2 == 1
+            t, half, which = later, nxt % 2, (nxt // 2 + 5 - slot) % 3
         outs = call(
-            lambda *refs, slab_end=slab_end, n=len(trans): middle_kernel(slab_end, n, *refs),
+            functools.partial(middle_kernel, slab_end, half),
             [FIELD] * (2 if slab_end else 1),
-            (which, inner, own, outer, *trans, rhi, rlo, chi, clo),
-            "slice",
-            scalar_first=True,
+            (which[None], inner, own, outer, *t, rhi, rlo, chi, clo),
+            scalars=1,
         )
         own = outs[0]
         if slab_end:
@@ -268,14 +274,14 @@
         )
         for n in range(3)
     ]
-    last = [permute(slabs[3], [(worker(k, p), home(3, p)) for p in range(TILES)]) for k in range(VIEWS)]
-    stored = [jnp.where(depth == 3, last[k], pick((depth + 3 - k) % 3, early)) for k in range(VIEWS)]
-    return jnp.stack([v.reshape(2, ROWS, COLS) for v in stored], axis=1)[:, :, None]
+    late = [permute(slabs[3], [(worker(k, p), home(SLABS - 1, p)) for p in range(TILES)]) for k in range(VIEWS)]
+    shape = jax.ShapeDtypeStruct((2, VIEWS, 1, ROWS, COLS), jnp.float32)
+    return call(assemble_kernel, shape, (depth[None], *early, *late), scalars=1, out_hbm=True)
 
 
 def solution(mesh):
     return jax.shard_map(
-        per_device,
+        propagate,
         mesh=mesh,
         in_specs=(
             P(None, None, "tile", None),

time: 152 us -> 119 us (0.78)
  the two profiles are of different devices: /device:TPU:7 before, /device:TPU:71 now
where the time goes in v2:
time: 119 us
  starting transfers between devices  65.6 us (55%)
  waiting for transfers between devices  45 us (38%)
  Pallas kernels  7.64 us (6%)
    ppermute x31, starting transfers between devices, permute(): return lax.ppermute(value, AXES, pairs)  65.6 us
    ppermute x31, waiting for transfers between devices, permute(): return lax.ppermute(value, AXES, pairs)  45 us
    pallas_call x11, Pallas kernels, call(): pl.pallas_call(kernel, out_shape=shapes, in_specs=specs, out_specs=jax.tr...  7.64 us
  transfers between devices with their start and end apart: 31, of which 16 were waited for; matrix products, arithmetic and copies ran while one was open for 0% of the time, Pallas kernels for 1%

profile of v2, /device:TPU:71, one launch (start us, length us, event | category | flops | bytes accessed | tf_op | source)
XLA Modules:
  0.0 118.9 jit_solution(17844896742505047148)
XLA Ops:
  0.0 1.7 %shard_map.73 = (f32[64,512]{1,0:T(8,128)S(1)}, f32[64,512]{1,0:T(8,128)S(1)}, f32[64,512]{1,0:T(8,128)S(1)}, f32[64,512]{1,0:T(8,128)S(1)}, f32[64,512]{1,0:T(8...) custom-call(s32[3]{0:T(128)} %order.1, ...), custom_call_target="tpu_custom_call" | custom-call | tf_op jit(solution)/shard_map/pallas_call | solution.py:203
  1.8 0.8 collective-permute-start
  2.6 0.7 collective-permute-start.1
  3.2 1.3 %collective-permute-start.2 = (f32[64,512]{1,0:T(8,128)S(1)}, f32[64,512]{1,0:T(8,128)S(1)}, u32[]{:S(2)}, u32[]{:S(2)}) collective-permute-start(f32[64,512]{1,0:T(8,128)S(1)} %get-tuple-element.22), channel_id=1, source_target_pairs={{0,128},{1,129},{2,130},{3,131},{4,195},{5,194},{6,193},{7,192},{8... | collective-permute-start | bytes 393224 | tf_op jit(solution)/shard_map/ppermute | solution.py:209
  4.5 0.7 collective-permute-start.5
  5.2 0.7 collective-permute-start.6
  5.9 1.3 %collective-permute-start.7 = (f32[64,512]{1,0:T(8,128)S(1)}, f32[64,512]{1,0:T(8,128)S(1)}, u32[]{:S(2)}, u32[]{:S(2)}) collective-permute-start(f32[64,512]{1,0:T(8,128)S(1)} %get-tuple-element.25), channel_id=1, source_target_pairs={{0,128},{1,129},{2,130},{3,131},{4,195},{5,194},{6,193},{7,192},{8... | collective-permute-start | bytes 393224 | tf_op jit(solution)/shard_map/ppermute | solution.py:209
  7.3 5.2 %collective-permute-start.10 = (f32[2,64,512]{2,1,0:T(8,128)S(1)}, f32[2,64,512]{2,1,0:T(8,128)S(1)}, u32[]{:S(2)}, u32[]{:S(2)}) collective-permute-start(f32[2,64,512]{2,1,0:T(8,128)S(1)} %get-tuple-element.26), channel_id=1, source_target_pairs={{64,0},{65,1},{66,2},{67,3},{68,67},{69,66},{70,65},{71,64},{72,8}... | collective-permute-start | bytes 786440 | tf_op jit(solution)/shard_map/ppermute | solution.py:209
  12.6 8.5 %collective-permute-done.2.c = f32[64,512]{1,0:T(8,128)S(1)} collective-permute-done((f32[64,512]{1,0:T(8,128)S(1)}, f32[64,512]{1,0:T(8,128)S(1)}, u32[]{:S(2)}, u32[]{:S(2)}) %collective-permute-start.2) | collective-permute-done | bytes 131104 | tf_op jit(solution)/shard_map/ppermute | solution.py:209
  21.1 4.9 %collective-permute-start.11 = (f32[2,64,512]{2,1,0:T(8,128)S(1)}, f32[2,64,512]{2,1,0:T(8,128)S(1)}, u32[]{:S(2)}, u32[]{:S(2)}) collective-permute-start(f32[2,64,512]{2,1,0:T(8,128)S(1)} %get-tuple-element.27), channel_id=1, source_target_pairs={{128,0},{129,1},{130,2},{131,3},{132,67},{133,66},{134,65},{135,64... | collective-permute-start | bytes 786440 | tf_op jit(solution)/shard_map/ppermute | solution.py:209
  26.5 1.9 %collective-permute-start.12 = (f32[2,64,512]{2,1,0:T(8,128)S(1)}, f32[2,64,512]{2,1,0:T(8,128)S(1)}, u32[]{:S(2)}, u32[]{:S(2)}) collective-permute-start(f32[2,64,512]{2,1,0:T(8,128)S(1)} %get-tuple-element.28), channel_id=1, source_target_pairs={{192,0},{193,1},{194,2},{195,3},{196,67},{197,66},{198,65},{199,64... | collective-permute-start | bytes 786440 | tf_op jit(solution)/shard_map/ppermute | solution.py:209
  28.5 0.8 collective-permute-start.4
  29.4 6.9 %collective-permute-done.3.inner = f32[64,512]{1,0:T(8,128)S(1)} collective-permute-done((f32[64,512]{1,0:T(8,128)S(1)}, f32[64,512]{1,0:T(8,128)S(1)}, u32[]{:S(2)}, u32[]{:S(2)}) %collective-permute-start.3) | collective-permute-done | bytes 131104 | tf_op jit(solution)/shard_map/ppermute | solution.py:209
  36.3 0.6 shard_map.75.own
  37.0 3.7 %collective-permute-start.9 = (f32[64,512]{1,0:T(8,128)S(1)}, f32[64,512]{1,0:T(8,128)S(1)}, u32[]{:S(2)}, u32[]{:S(2)}) collective-permute-start(f32[64,512]{1,0:T(8,128)S(1)} %shard_map.75.own), channel_id=1, source_target_pairs={{0,96},{1,2},{2,1},{3,67},{67,3},{66,65},{65,66},{64,8},{8,64},{9,... | collective-permute-start | bytes 393224 | tf_op jit(solution)/shard_map/ppermute | solution.py:209
  40.7 0.7 collective-permute-done.12.refs_2_
  41.4 3.4 %collective-permute-done.8.inner = f32[64,512]{1,0:T(8,128)S(1)} collective-permute-done((f32[64,512]{1,0:T(8,128)S(1)}, f32[64,512]{1,0:T(8,128)S(1)}, u32[]{:S(2)}, u32[]{:S(2)}) %collective-permute-start.8) | collective-permute-done | bytes 131104 | tf_op jit(solution)/shard_map/ppermute | solution.py:209
  44.8 0.6 shard_map.76
  45.5 4.0 %collective-permute-start.13 = (f32[64,512]{1,0:T(8,128)S(1)}, f32[64,512]{1,0:T(8,128)S(1)}, u32[]{:S(2)}, u32[]{:S(2)}) collective-permute-start(f32[64,512]{1,0:T(8,128)S(1)} %get-tuple-element.29.own), channel_id=1, source_target_pairs={{0,1},{1,0},{2,3},{3,2},{67,66},{66,67},{65,64},{64,65},{8,9},{9,8... | collective-permute-start | bytes 393224 | tf_op jit(solution)/shard_map/ppermute | solution.py:209
  49.4 0.8 collective-permute-start.14
  50.2 1.9 %collective-permute-done.13.inner = f32[64,512]{1,0:T(8,128)S(1)} collective-permute-done((f32[64,512]{1,0:T(8,128)S(1)}, f32[64,512]{1,0:T(8,128)S(1)}, u32[]{:S(2)}, u32[]{:S(2)}) %collective-permute-start.13) | collective-permute-done | bytes 131104 | tf_op jit(solution)/shard_map/ppermute | solution.py:209
  52.1 1.2 collective-permute-done.14.outer
  53.3 0.6 shard_map.77.own
  54.0 1.6 %collective-permute-start.16 = (f32[64,512]{1,0:T(8,128)S(1)}, f32[64,512]{1,0:T(8,128)S(1)}, u32[]{:S(2)}, u32[]{:S(2)}) collective-permute-start(f32[64,512]{1,0:T(8,128)S(1)} %shard_map.77.own), channel_id=1, source_target_pairs={{0,96},{1,2},{2,1},{3,67},{67,3},{66,65},{65,66},{64,8},{8,64},{9,... | collective-permute-start | bytes 393224 | tf_op jit(solution)/shard_map/ppermute | solution.py:209
  55.6 3.7 %collective-permute-done.15.inner = f32[64,512]{1,0:T(8,128)S(1)} collective-permute-done((f32[64,512]{1,0:T(8,128)S(1)}, f32[64,512]{1,0:T(8,128)S(1)}, u32[]{:S(2)}, u32[]{:S(2)}) %collective-permute-start.15) | collective-permute-done | bytes 131104 | tf_op jit(solution)/shard_map/ppermute | solution.py:209
  59.4 0.6 shard_map.78
  60.2 1.9 %collective-permute-start.18 = (f32[64,512]{1,0:T(8,128)S(1)}, f32[64,512]{1,0:T(8,128)S(1)}, u32[]{:S(2)}, u32[]{:S(2)}) collective-permute-start(f32[64,512]{1,0:T(8,128)S(1)} %get-tuple-element.30.own), channel_id=1, source_target_pairs={{0,96},{1,2},{2,1},{3,67},{67,3},{66,65},{65,66},{64,8},{8,64},{9,... | collective-permute-start | bytes 393224 | tf_op jit(solution)/shard_map/ppermute | solution.py:209
  62.1 2.4 %collective-permute-done.17.inner = f32[64,512]{1,0:T(8,128)S(1)} collective-permute-done((f32[64,512]{1,0:T(8,128)S(1)}, f32[64,512]{1,0:T(8,128)S(1)}, u32[]{:S(2)}, u32[]{:S(2)}) %collective-permute-start.17) | collective-permute-done | bytes 131104 | tf_op jit(solution)/shard_map/ppermute | solution.py:209
  64.6 0.8 collective-permute-done.18.outer
  65.4 0.6 shard_map.79.own
  66.1 2.1 %collective-permute-start.20 = (f32[64,512]{1,0:T(8,128)S(1)}, f32[64,512]{1,0:T(8,128)S(1)}, u32[]{:S(2)}, u32[]{:S(2)}) collective-permute-start(f32[64,512]{1,0:T(8,128)S(1)} %shard_map.79.own), channel_id=1, source_target_pairs={{0,96},{1,2},{2,1},{3,67},{67,3},{66,65},{65,66},{64,8},{8,64},{9,... | collective-permute-start | bytes 393224 | tf_op jit(solution)/shard_map/ppermute | solution.py:209
  68.2 1.7 %collective-permute-done.19.inner = f32[64,512]{1,0:T(8,128)S(1)} collective-permute-done((f32[64,512]{1,0:T(8,128)S(1)}, f32[64,512]{1,0:T(8,128)S(1)}, u32[]{:S(2)}, u32[]{:S(2)}) %collective-permute-start.19) | collective-permute-done | bytes 131104 | tf_op jit(solution)/shard_map/ppermute | solution.py:209
  69.9 1.0 collective-permute-done.20.outer
  70.9 0.6 shard_map.80
  71.7 2.9 %collective-permute-start.25 = (f32[64,512]{1,0:T(8,128)S(1)}, f32[64,512]{1,0:T(8,128)S(1)}, u32[]{:S(2)}, u32[]{:S(2)}) collective-permute-start(f32[64,512]{1,0:T(8,128)S(1)} %get-tuple-element.34.own), channel_id=1, source_target_pairs={{0,96},{1,2},{2,1},{3,67},{67,3},{66,65},{65,66},{64,8},{8,64},{9,... | collective-permute-start | bytes 393224 | tf_op jit(solution)/shard_map/ppermute | solution.py:209
  74.6 0.9 collective-permute-done.24.inner
  75.5 1.8 %collective-permute-done.25.outer = f32[64,512]{1,0:T(8,128)S(1)} collective-permute-done((f32[64,512]{1,0:T(8,128)S(1)}, f32[64,512]{1,0:T(8,128)S(1)}, u32[]{:S(2)}, u32[]{:S(2)}) %collective-permute-start.25) | collective-permute-done | bytes 131104 | tf_op jit(solution)/shard_map/ppermute | solution.py:209
  77.2 0.6 shard_map.81.own
  78.0 3.4 %collective-permute-start.27 = (f32[64,512]{1,0:T(8,128)S(1)}, f32[64,512]{1,0:T(8,128)S(1)}, u32[]{:S(2)}, u32[]{:S(2)}) collective-permute-start(f32[64,512]{1,0:T(8,128)S(1)} %shard_map.81.own), channel_id=1, source_target_pairs={{0,96},{1,2},{2,1},{3,67},{67,3},{66,65},{65,66},{64,8},{8,64},{9,... | collective-permute-start | bytes 393224 | tf_op jit(solution)/shard_map/ppermute | solution.py:209
  81.5 7.5 %collective-permute-start.21 = (f32[64,512]{1,0:T(8,128)S(1)}, f32[64,512]{1,0:T(8,128)S(1)}, u32[]{:S(2)}, u32[]{:S(2)}) collective-permute-start(f32[64,512]{1,0:T(8,128)S(1)} %get-tuple-element.37), channel_id=1, source_target_pairs={{0,0},{1,1},{2,2},{3,3},{67,4},{66,5},{65,6},{64,7},{8,8},{9,9},{1... | collective-permute-start | bytes 393224 | tf_op jit(solution)/shard_map/ppermute | solution.py:209
  89.0 1.3 %collective-permute-start.22 = (f32[64,512]{1,0:T(8,128)S(1)}, f32[64,512]{1,0:T(8,128)S(1)}, u32[]{:S(2)}, u32[]{:S(2)}) collective-permute-start(f32[64,512]{1,0:T(8,128)S(1)} %get-tuple-element.36), channel_id=1, source_target_pairs={{0,64},{1,65},{2,66},{3,67},{67,68},{66,69},{65,70},{64,71},{8,72}... | collective-permute-start | bytes 393224 | tf_op jit(solution)/shard_map/ppermute | solution.py:209
  90.3 13.0 %collective-permute-start.23 = (f32[64,512]{1,0:T(8,128)S(1)}, f32[64,512]{1,0:T(8,128)S(1)}, u32[]{:S(2)}, u32[]{:S(2)}) collective-permute-start(f32[64,512]{1,0:T(8,128)S(1)} %get-tuple-element.35), channel_id=1, source_target_pairs={{0,128},{1,129},{2,130},{3,131},{67,132},{66,133},{65,134},{64,135... | collective-permute-start | bytes 393224 | tf_op jit(solution)/shard_map/ppermute | solution.py:209
  103.5 1.3 %collective-permute-start.28 = (f32[64,512]{1,0:T(8,128)S(1)}, f32[64,512]{1,0:T(8,128)S(1)}, u32[]{:S(2)}, u32[]{:S(2)}) collective-permute-start(f32[64,512]{1,0:T(8,128)S(1)} %shard_map.82), channel_id=1, source_target_pairs={{0,192},{1,193},{2,194},{3,195},{67,196},{66,197},{65,198},{64,199... | collective-permute-start | bytes 393224 | tf_op jit(solution)/shard_map/ppermute | solution.py:209
  104.8 1.3 %collective-permute-start.29 = (f32[64,512]{1,0:T(8,128)S(1)}, f32[64,512]{1,0:T(8,128)S(1)}, u32[]{:S(2)}, u32[]{:S(2)}) collective-permute-start(f32[64,512]{1,0:T(8,128)S(1)} %shard_map.82), channel_id=1, source_target_pairs={{71,192},{70,193},{69,194},{68,195},{4,196},{5,197},{6,198},{7,199... | collective-permute-start | bytes 393224 | tf_op jit(solution)/shard_map/ppermute | solution.py:209
  106.1 1.9 %collective-permute-start.30 = (f32[64,512]{1,0:T(8,128)S(1)}, f32[64,512]{1,0:T(8,128)S(1)}, u32[]{:S(2)}, u32[]{:S(2)}) collective-permute-start(f32[64,512]{1,0:T(8,128)S(1)} %shard_map.82), channel_id=1, source_target_pairs={{128,192},{129,193},{130,194},{131,195},{195,196},{194,197},{193,1... | collective-permute-start | bytes 393224 | tf_op jit(solution)/shard_map/ppermute | solution.py:209
  108.1 5.4 %collective-permute-done.28.refs_3_ = f32[64,512]{1,0:T(8,128)S(1)} collective-permute-done((f32[64,512]{1,0:T(8,128)S(1)}, f32[64,512]{1,0:T(8,128)S(1)}, u32[]{:S(2)}, u32[]{:S(2)}) %collective-permute-start.28) | collective-permute-done | bytes 131104 | tf_op jit(solution)/shard_map/ppermute | solution.py:209
  113.5 4.5 %collective-permute-done.29.refs_4_ = f32[64,512]{1,0:T(8,128)S(1)} collective-permute-done((f32[64,512]{1,0:T(8,128)S(1)}, f32[64,512]{1,0:T(8,128)S(1)}, u32[]{:S(2)}, u32[]{:S(2)}) %collective-permute-start.29) | collective-permute-done | bytes 131104 | tf_op jit(solution)/shard_map/ppermute | solution.py:209
  118.1 0.8 shard_map.83
  (40 shorter events, 1.5 us)
Async XLA Ops:
  0.0 26.0 %copy-start.1 = (bf16[384,256]{1,0:T(8,128)(2,1)S(1)}, bf16[384,256]{1,0:T(8,128)(2,1)}, u32[]{:S(2)}) copy-start(bf16[384,256]{1,0:T(8,128)(2,1)} %constant.138.clo.refs_6_) | copy-start | bytes 589828
  1.7 24.3 %copy-start = (bf16[384,256]{1,0:T(8,128)(2,1)S(1)}, bf16[384,256]{1,0:T(8,128)(2,1)}, u32[]{:S(2)}) copy-start(bf16[384,256]{1,0:T(8,128)(2,1)} %constant.135.chi.refs_5_) | copy-start | bytes 589828
  1.8 4.1 %collective-permute-start = (f32[64,512]{1,0:T(8,128)S(1)}, f32[64,512]{1,0:T(8,128)S(1)}, u32[]{:S(2)}, u32[]{:S(2)}) collective-permute-start(f32[64,512]{1,0:T(8,128)S(1)} %get-tuple-element.20), channel_id=1, source_target_pairs={{0,0},{1,1},{2,2},{3,3},{4,67},{5,66},{6,65},{7,64},{8,8},{9,9},{1... | collective-permute-start | bytes 393224 | tf_op jit(solution)/shard_map/ppermute | solution.py:209
  2.6 4.8 %collective-permute-start.1 = (f32[64,512]{1,0:T(8,128)S(1)}, f32[64,512]{1,0:T(8,128)S(1)}, u32[]{:S(2)}, u32[]{:S(2)}) collective-permute-start(f32[64,512]{1,0:T(8,128)S(1)} %get-tuple-element.21), channel_id=1, source_target_pairs={{0,71},{1,70},{2,69},{3,68},{4,4},{5,5},{6,6},{7,7},{8,79},{9,78},... | collective-permute-start | bytes 393224 | tf_op jit(solution)/shard_map/ppermute | solution.py:209
  3.2 17.9 %collective-permute-start.2 = (f32[64,512]{1,0:T(8,128)S(1)}, f32[64,512]{1,0:T(8,128)S(1)}, u32[]{:S(2)}, u32[]{:S(2)}) collective-permute-start(f32[64,512]{1,0:T(8,128)S(1)} %get-tuple-element.22), channel_id=1, source_target_pairs={{0,128},{1,129},{2,130},{3,131},{4,195},{5,194},{6,193},{7,192},{8... | collective-permute-start | bytes 393224 | tf_op jit(solution)/shard_map/ppermute | solution.py:209
  4.5 21.9 %collective-permute-start.5 = (f32[64,512]{1,0:T(8,128)S(1)}, f32[64,512]{1,0:T(8,128)S(1)}, u32[]{:S(2)}, u32[]{:S(2)}) collective-permute-start(f32[64,512]{1,0:T(8,128)S(1)} %get-tuple-element.23), channel_id=1, source_target_pairs={{0,0},{1,1},{2,2},{3,3},{4,67},{5,66},{6,65},{7,64},{8,8},{9,9},{1... | collective-permute-start | bytes 393224 | tf_op jit(solution)/shard_map/ppermute | solution.py:209
  5.2 23.2 %collective-permute-start.6 = (f32[64,512]{1,0:T(8,128)S(1)}, f32[64,512]{1,0:T(8,128)S(1)}, u32[]{:S(2)}, u32[]{:S(2)}) collective-permute-start(f32[64,512]{1,0:T(8,128)S(1)} %get-tuple-element.24), channel_id=1, source_target_pairs={{0,71},{1,70},{2,69},{3,68},{4,4},{5,5},{6,6},{7,7},{8,79},{9,78},... | collective-permute-start | bytes 393224 | tf_op jit(solution)/shard_map/ppermute | solution.py:209
  5.9 22.6 %collective-permute-start.7 = (f32[64,512]{1,0:T(8,128)S(1)}, f32[64,512]{1,0:T(8,128)S(1)}, u32[]{:S(2)}, u32[]{:S(2)}) collective-permute-start(f32[64,512]{1,0:T(8,128)S(1)} %get-tuple-element.25), channel_id=1, source_target_pairs={{0,128},{1,129},{2,130},{3,131},{4,195},{5,194},{6,193},{7,192},{8... | collective-permute-start | bytes 393224 | tf_op jit(solution)/shard_map/ppermute | solution.py:209
  7.3 33.3 %collective-permute-start.10 = (f32[2,64,512]{2,1,0:T(8,128)S(1)}, f32[2,64,512]{2,1,0:T(8,128)S(1)}, u32[]{:S(2)}, u32[]{:S(2)}) collective-permute-start(f32[2,64,512]{2,1,0:T(8,128)S(1)} %get-tuple-element.26), channel_id=1, source_target_pairs={{64,0},{65,1},{66,2},{67,3},{68,67},{69,66},{70,65},{71,64},{72,8}... | collective-permute-start | bytes 786440 | tf_op jit(solution)/shard_map/ppermute | solution.py:209
  21.1 8.3 %copy-start.2 = (bf16[64,192]{1,0:T(8,128)(2,1)S(1)}, bf16[64,192]{1,0:T(8,128)(2,1)}, u32[]{:S(2)}) copy-start(bf16[64,192]{1,0:T(8,128)(2,1)} %constant.143) | copy-start | bytes 73732
  21.1 8.3 %copy-start.3 = (bf16[64,192]{1,0:T(8,128)(2,1)S(1)}, bf16[64,192]{1,0:T(8,128)(2,1)}, u32[]{:S(2)}) copy-start(bf16[64,192]{1,0:T(8,128)(2,1)} %constant.146) | copy-start | bytes 73732
  21.1 8.3 %copy-start.4 = (bf16[64,192]{1,0:T(8,128)(2,1)S(1)}, bf16[64,192]{1,0:T(8,128)(2,1)}, u32[]{:S(2)}) copy-start(bf16[64,192]{1,0:T(8,128)(2,1)} %constant.139) | copy-start | bytes 73732
  21.1 8.3 %copy-start.5 = (bf16[64,192]{1,0:T(8,128)(2,1)S(1)}, bf16[64,192]{1,0:T(8,128)(2,1)}, u32[]{:S(2)}) copy-start(bf16[64,192]{1,0:T(8,128)(2,1)} %constant.140) | copy-start | bytes 73732
  21.1 19.6 %collective-permute-start.11 = (f32[2,64,512]{2,1,0:T(8,128)S(1)}, f32[2,64,512]{2,1,0:T(8,128)S(1)}, u32[]{:S(2)}, u32[]{:S(2)}) collective-permute-start(f32[2,64,512]{2,1,0:T(8,128)S(1)} %get-tuple-element.27), channel_id=1, source_target_pairs={{128,0},{129,1},{130,2},{131,3},{132,67},{133,66},{134,65},{135,64... | collective-permute-start | bytes 786440 | tf_op jit(solution)/shard_map/ppermute | solution.py:209
  26.5 15.0 %collective-permute-start.12 = (f32[2,64,512]{2,1,0:T(8,128)S(1)}, f32[2,64,512]{2,1,0:T(8,128)S(1)}, u32[]{:S(2)}, u32[]{:S(2)}) collective-permute-start(f32[2,64,512]{2,1,0:T(8,128)S(1)} %get-tuple-element.28), channel_id=1, source_target_pairs={{192,0},{193,1},{194,2},{195,3},{196,67},{197,66},{198,65},{199,64... | collective-permute-start | bytes 786440 | tf_op jit(solution)/shard_map/ppermute | solution.py:209
  28.4 7.9 %collective-permute-start.3 = (f32[64,512]{1,0:T(8,128)S(1)}, f32[64,512]{1,0:T(8,128)S(1)}, u32[]{:S(2)}, u32[]{:S(2)}) collective-permute-start(f32[64,512]{1,0:T(8,128)S(1)} %shard_map.74.own), channel_id=1, source_target_pairs={{0,1},{1,0},{2,3},{3,2},{67,66},{66,67},{65,64},{64,65},{8,9},{9,8... | collective-permute-start | bytes 393224 | tf_op jit(solution)/shard_map/ppermute | solution.py:209
  28.5 7.8 %collective-permute-start.4 = (f32[64,512]{1,0:T(8,128)S(1)}, f32[64,512]{1,0:T(8,128)S(1)}, u32[]{:S(2)}, u32[]{:S(2)}) collective-permute-start(f32[64,512]{1,0:T(8,128)S(1)} %shard_map.74.own), channel_id=1, source_target_pairs={{0,96},{1,2},{2,1},{3,67},{67,3},{66,65},{65,66},{64,8},{8,64},{9,... | collective-permute-start | bytes 393224 | tf_op jit(solution)/shard_map/ppermute | solution.py:209
  36.9 7.9 %collective-permute-start.8 = (f32[64,512]{1,0:T(8,128)S(1)}, f32[64,512]{1,0:T(8,128)S(1)}, u32[]{:S(2)}, u32[]{:S(2)}) collective-permute-start(f32[64,512]{1,0:T(8,128)S(1)} %shard_map.75.own), channel_id=1, source_target_pairs={{0,1},{1,0},{2,3},{3,2},{67,66},{66,67},{65,64},{64,65},{8,9},{9,8... | collective-permute-start | bytes 393224 | tf_op jit(solution)/shard_map/ppermute | solution.py:209
  37.0 7.8 %collective-permute-start.9 = (f32[64,512]{1,0:T(8,128)S(1)}, f32[64,512]{1,0:T(8,128)S(1)}, u32[]{:S(2)}, u32[]{:S(2)}) collective-permute-start(f32[64,512]{1,0:T(8,128)S(1)} %shard_map.75.own), channel_id=1, source_target_pairs={{0,96},{1,2},{2,1},{3,67},{67,3},{66,65},{65,66},{64,8},{8,64},{9,... | collective-permute-start | bytes 393224 | tf_op jit(solution)/shard_map/ppermute | solution.py:209
  45.5 6.6 %collective-permute-start.13 = (f32[64,512]{1,0:T(8,128)S(1)}, f32[64,512]{1,0:T(8,128)S(1)}, u32[]{:S(2)}, u32[]{:S(2)}) collective-permute-start(f32[64,512]{1,0:T(8,128)S(1)} %get-tuple-element.29.own), channel_id=1, source_target_pairs={{0,1},{1,0},{2,3},{3,2},{67,66},{66,67},{65,64},{64,65},{8,9},{9,8... | collective-permute-start | bytes 393224 | tf_op jit(solution)/shard_map/ppermute | solution.py:209
  49.4 3.8 %collective-permute-start.14 = (f32[64,512]{1,0:T(8,128)S(1)}, f32[64,512]{1,0:T(8,128)S(1)}, u32[]{:S(2)}, u32[]{:S(2)}) collective-permute-start(f32[64,512]{1,0:T(8,128)S(1)} %get-tuple-element.29.own), channel_id=1, source_target_pairs={{0,96},{1,2},{2,1},{3,67},{67,3},{66,65},{65,66},{64,8},{8,64},{9,... | collective-permute-start | bytes 393224 | tf_op jit(solution)/shard_map/ppermute | solution.py:209
  53.9 5.5 %collective-permute-start.15 = (f32[64,512]{1,0:T(8,128)S(1)}, f32[64,512]{1,0:T(8,128)S(1)}, u32[]{:S(2)}, u32[]{:S(2)}) collective-permute-start(f32[64,512]{1,0:T(8,128)S(1)} %shard_map.77.own), channel_id=1, source_target_pairs={{0,1},{1,0},{2,3},{3,2},{67,66},{66,67},{65,64},{64,65},{8,9},{9,8... | collective-permute-start | bytes 393224 | tf_op jit(solution)/shard_map/ppermute | solution.py:209
  54.0 5.4 %collective-permute-start.16 = (f32[64,512]{1,0:T(8,128)S(1)}, f32[64,512]{1,0:T(8,128)S(1)}, u32[]{:S(2)}, u32[]{:S(2)}) collective-permute-start(f32[64,512]{1,0:T(8,128)S(1)} %shard_map.77.own), channel_id=1, source_target_pairs={{0,96},{1,2},{2,1},{3,67},{67,3},{66,65},{65,66},{64,8},{8,64},{9,... | collective-permute-start | bytes 393224 | tf_op jit(solution)/shard_map/ppermute | solution.py:209
  60.1 4.5 %collective-permute-start.17 = (f32[64,512]{1,0:T(8,128)S(1)}, f32[64,512]{1,0:T(8,128)S(1)}, u32[]{:S(2)}, u32[]{:S(2)}) collective-permute-start(f32[64,512]{1,0:T(8,128)S(1)} %get-tuple-element.30.own), channel_id=1, source_target_pairs={{0,1},{1,0},{2,3},{3,2},{67,66},{66,67},{65,64},{64,65},{8,9},{9,8... | collective-permute-start | bytes 393224 | tf_op jit(solution)/shard_map/ppermute | solution.py:209
  60.2 5.2 %collective-permute-start.18 = (f32[64,512]{1,0:T(8,128)S(1)}, f32[64,512]{1,0:T(8,128)S(1)}, u32[]{:S(2)}, u32[]{:S(2)}) collective-permute-start(f32[64,512]{1,0:T(8,128)S(1)} %get-tuple-element.30.own), channel_id=1, source_target_pairs={{0,96},{1,2},{2,1},{3,67},{67,3},{66,65},{65,66},{64,8},{8,64},{9,... | collective-permute-start | bytes 393224 | tf_op jit(solution)/shard_map/ppermute | solution.py:209
  66.0 3.9 %collective-permute-start.19 = (f32[64,512]{1,0:T(8,128)S(1)}, f32[64,512]{1,0:T(8,128)S(1)}, u32[]{:S(2)}, u32[]{:S(2)}) collective-permute-start(f32[64,512]{1,0:T(8,128)S(1)} %shard_map.79.own), channel_id=1, source_target_pairs={{0,1},{1,0},{2,3},{3,2},{67,66},{66,67},{65,64},{64,65},{8,9},{9,8... | collective-permute-start | bytes 393224 | tf_op jit(solution)/shard_map/ppermute | solution.py:209
  66.1 4.8 %collective-permute-start.20 = (f32[64,512]{1,0:T(8,128)S(1)}, f32[64,512]{1,0:T(8,128)S(1)}, u32[]{:S(2)}, u32[]{:S(2)}) collective-permute-start(f32[64,512]{1,0:T(8,128)S(1)} %shard_map.79.own), channel_id=1, source_target_pairs={{0,96},{1,2},{2,1},{3,67},{67,3},{66,65},{65,66},{64,8},{8,64},{9,... | collective-permute-start | bytes 393224 | tf_op jit(solution)/shard_map/ppermute | solution.py:209
  71.6 3.9 %collective-permute-start.24 = (f32[64,512]{1,0:T(8,128)S(1)}, f32[64,512]{1,0:T(8,128)S(1)}, u32[]{:S(2)}, u32[]{:S(2)}) collective-permute-start(f32[64,512]{1,0:T(8,128)S(1)} %get-tuple-element.34.own), channel_id=1, source_target_pairs={{0,1},{1,0},{2,3},{3,2},{67,66},{66,67},{65,64},{64,65},{8,9},{9,8... | collective-permute-start | bytes 393224 | tf_op jit(solution)/shard_map/ppermute | solution.py:209
  71.7 5.6 %collective-permute-start.25 = (f32[64,512]{1,0:T(8,128)S(1)}, f32[64,512]{1,0:T(8,128)S(1)}, u32[]{:S(2)}, u32[]{:S(2)}) collective-permute-start(f32[64,512]{1,0:T(8,128)S(1)} %get-tuple-element.34.own), channel_id=1, source_target_pairs={{0,96},{1,2},{2,1},{3,67},{67,3},{66,65},{65,66},{64,8},{8,64},{9,... | collective-permute-start | bytes 393224 | tf_op jit(solution)/shard_map/ppermute | solution.py:209
  77.9 25.4 %collective-permute-start.26 = (f32[64,512]{1,0:T(8,128)S(1)}, f32[64,512]{1,0:T(8,128)S(1)}, u32[]{:S(2)}, u32[]{:S(2)}) collective-permute-start(f32[64,512]{1,0:T(8,128)S(1)} %shard_map.81.own), channel_id=1, source_target_pairs={{0,1},{1,0},{2,3},{3,2},{67,66},{66,67},{65,64},{64,65},{8,9},{9,8... | collective-permute-start | bytes 393224 | tf_op jit(solution)/shard_map/ppermute | solution.py:209
  78.0 25.3 %collective-permute-start.27 = (f32[64,512]{1,0:T(8,128)S(1)}, f32[64,512]{1,0:T(8,128)S(1)}, u32[]{:S(2)}, u32[]{:S(2)}) collective-permute-start(f32[64,512]{1,0:T(8,128)S(1)} %shard_map.81.own), channel_id=1, source_target_pairs={{0,96},{1,2},{2,1},{3,67},{67,3},{66,65},{65,66},{64,8},{8,64},{9,... | collective-permute-start | bytes 393224 | tf_op jit(solution)/shard_map/ppermute | solution.py:209
  81.5 24.7 %collective-permute-start.21 = (f32[64,512]{1,0:T(8,128)S(1)}, f32[64,512]{1,0:T(8,128)S(1)}, u32[]{:S(2)}, u32[]{:S(2)}) collective-permute-start(f32[64,512]{1,0:T(8,128)S(1)} %get-tuple-element.37), channel_id=1, source_target_pairs={{0,0},{1,1},{2,2},{3,3},{67,4},{66,5},{65,6},{64,7},{8,8},{9,9},{1... | collective-permute-start | bytes 393224 | tf_op jit(solution)/shard_map/ppermute | solution.py:209
  89.0 19.1 %collective-permute-start.22 = (f32[64,512]{1,0:T(8,128)S(1)}, f32[64,512]{1,0:T(8,128)S(1)}, u32[]{:S(2)}, u32[]{:S(2)}) collective-permute-start(f32[64,512]{1,0:T(8,128)S(1)} %get-tuple-element.36), channel_id=1, source_target_pairs={{0,64},{1,65},{2,66},{3,67},{67,68},{66,69},{65,70},{64,71},{8,72}... | collective-permute-start | bytes 393224 | tf_op jit(solution)/shard_map/ppermute | solution.py:209
  90.3 17.8 %collective-permute-start.23 = (f32[64,512]{1,0:T(8,128)S(1)}, f32[64,512]{1,0:T(8,128)S(1)}, u32[]{:S(2)}, u32[]{:S(2)}) collective-permute-start(f32[64,512]{1,0:T(8,128)S(1)} %get-tuple-element.35), channel_id=1, source_target_pairs={{0,128},{1,129},{2,130},{3,131},{67,132},{66,133},{65,134},{64,135... | collective-permute-start | bytes 393224 | tf_op jit(solution)/shard_map/ppermute | solution.py:209
  103.5 10.0 %collective-permute-start.28 = (f32[64,512]{1,0:T(8,128)S(1)}, f32[64,512]{1,0:T(8,128)S(1)}, u32[]{:S(2)}, u32[]{:S(2)}) collective-permute-start(f32[64,512]{1,0:T(8,128)S(1)} %shard_map.82), channel_id=1, source_target_pairs={{0,192},{1,193},{2,194},{3,195},{67,196},{66,197},{65,198},{64,199... | collective-permute-start | bytes 393224 | tf_op jit(solution)/shard_map/ppermute | solution.py:209
  104.8 13.2 %collective-permute-start.29 = (f32[64,512]{1,0:T(8,128)S(1)}, f32[64,512]{1,0:T(8,128)S(1)}, u32[]{:S(2)}, u32[]{:S(2)}) collective-permute-start(f32[64,512]{1,0:T(8,128)S(1)} %shard_map.82), channel_id=1, source_target_pairs={{71,192},{70,193},{69,194},{68,195},{4,196},{5,197},{6,198},{7,199... | collective-permute-start | bytes 393224 | tf_op jit(solution)/shard_map/ppermute | solution.py:209
  106.1 11.9 %collective-permute-start.30 = (f32[64,512]{1,0:T(8,128)S(1)}, f32[64,512]{1,0:T(8,128)S(1)}, u32[]{:S(2)}, u32[]{:S(2)}) collective-permute-start(f32[64,512]{1,0:T(8,128)S(1)} %shard_map.82), channel_id=1, source_target_pairs={{128,192},{129,193},{130,194},{131,195},{195,196},{194,197},{193,1... | collective-permute-start | bytes 393224 | tf_op jit(solution)/shard_map/ppermute | solution.py:209

commit v3 on v2

--- a/solution.py
+++ b/solution.py
@@ -22,16 +22,43 @@
     return ((x // 2) * 2 + core) * TILES + (x % 2) * 32 + y * 8 + z
 
 
+def flipped(slot):
+    return 1 - slot % 2
+
+
 def worker(slot, tile):
     x_lo, rest = divmod(tile, 32)
     y, z = divmod(rest, 8)
-    y = y if x_lo == 0 else 3 - y
+    y = 3 - y if x_lo == flipped(slot) else y
     core = 0 if z // 4 == slot % 2 else 1
     return device_at(2 * (slot // 2) + x_lo, y, z if core == 0 else 7 - z, core)
 
 
 def home(depth, tile):
     return depth * TILES + tile
+
+
+def place_of(device):
+    depth, tile = divmod(device, TILES)
+    return 2 * (depth // 2) + tile // 32, tile % 32 // 8, tile % 8, depth % 2
+
+
+def distance(a, b):
+    (ax, ay, az, ac), (bx, by, bz, bc) = place_of(a), place_of(b)
+    hops = [min((p - q) % n, (q - p) % n) for p, q, n in ((ax, bx, 4), (ay, by, 4), (az, bz, 8))]
+    return 4 * sum(hops) + abs(ac - bc)
+
+
+def completed(pairs):
+    sources = sorted(set(range(SLABS * TILES)) - {a for a, _ in pairs})
+    targets = sorted(set(range(SLABS * TILES)) - {b for _, b in pairs})
+    extra = []
+    for a, b in sorted(((a, b) for a in sources for b in targets), key=lambda ab: (distance(*ab), ab)):
+        if a in sources and b in targets:
+            sources.remove(a)
+            targets.remove(b)
+            extra.append((a, b))
+    return list(pairs) + extra
 
 
 INNER = [(worker(k, p), worker(k, p ^ 1)) for k in range(4) for p in range(TILES)]
@@ -40,6 +67,21 @@
     for k in range(4)
     for p in range(TILES)
 ]
+
+
+GIVES = [
+    {0: 0, 1: 1},
+    {1: 0, 2: 1},
+    {2: 0, 0: 1, 1: 2},
+    {0: 3, 2: 2},
+    {1: 3, 0: 2},
+    {2: 3},
+]
+FIRST = [0, 1]
+
+
+def ready(slab):
+    return [give for give in GIVES if max(give.values()) == slab]
 
 
 def taps():
@@ -146,53 +188,81 @@
     return out
 
 
+def turn(slot):
+    return (slot + 1) % VIEWS
+
+
 def prepare_kernel(order, depth, incident, delta, beta, *outs):
-    @pl.when(depth[0] == 0)
-    def _():
-        for slot in range(VIEWS):
-            view = order[slot]
-            entering = jnp.concatenate([incident[0, view], incident[1, view]], axis=0)
-            outs[slot][...] = times(transmission(delta[view, 0], beta[view, 0]), entering)
-            outs[VIEWS + slot][...] = transmission(delta[view, 1], beta[view, 1])
-
-    @pl.when(depth[0] > 0)
-    def _():
-        for m in range(VIEWS):
-            view = order[lax.rem(depth[0] + 5 - m, 3)]
-            for half in range(2):
-                outs[2 * VIEWS + m][half] = transmission(delta[view, half], beta[view, half])
-
-
-def first_kernel(a, b, c, chi, clo, out):
-    out[...] = column_blur(a[...] + b[...] + c[...], chi[...], clo[...])
-
-
-def middle_kernel(slab_end, half, which, inner, own, outer, *refs):
-    trans, (rhi, rlo, chi, clo), outs = refs[:VIEWS], refs[VIEWS : VIEWS + 4], refs[VIEWS + 4 :]
+    for m in range(SLABS):
+        step = lax.rem(m + SLABS - depth[0], SLABS)
+
+        @pl.when(step < VIEWS)
+        def _(m=m, step=step):
+            view = order[lax.rem(step + VIEWS - 1, VIEWS)]
+            first = transmission(delta[view, 0], beta[view, 0])
+            outs[m][0] = first
+            outs[m][1] = transmission(delta[view, 1], beta[view, 1])
+
+            @pl.when(depth[0] == 0)
+            def _():
+                entering = jnp.concatenate([incident[0, view], incident[1, view]], axis=0)
+                outs[m][0] = times(first, entering)
+                for n, k in enumerate(FIRST):
+                    if turn(k) == m:
+                        outs[SLABS + n][...] = times(first, entering)
+
+
+def first_kernel(slot, *refs):
+    fields, (chi, clo, out) = refs[:VIEWS], refs[VIEWS:]
+    field = pick(slot[0], [f[...] if k in FIRST else f[0] for k, f in enumerate(fields)])
+    out[...] = column_blur(field, chi[...], clo[...])
+
+
+def give_out(which, slabs, outs):
+    for give, out in zip(ready(len(slabs) - 1), outs, strict=True):
+        some = next(iter(give.values()))
+        out[...] = pick(which, [slabs[give.get(k, some)] for k in range(VIEWS)])
+
+
+def middle_kernel(piece, slot, inner, own, outer, *refs):
+    slab_end = piece % 2 == 1
+    nxt = piece + 1
+    done = piece // 2 if slab_end else 0
+    older, refs = refs[:done], refs[done:]
+    trans, (rhi, rlo, chi, clo), outs = refs[:SLABS], refs[SLABS : SLABS + 4], refs[SLABS + 4 :]
     field = row_blur(inner[...], own[...], outer[...], rhi[...], rlo[...])
+    which = lax.rem(lax.rem(slot[0] + 1, VIEWS) + nxt // 2, SLABS)
+    t = pick(which, [r[nxt % 2] for r in trans])
+    outs[0][...] = column_blur(times(t, field), chi[...], clo[...])
     if slab_end:
         outs[1][...] = field
-    t = pick(which[0], [r[...] if half is None else r[half] for r in trans])
-    outs[0][...] = column_blur(times(t, field), chi[...], clo[...])
-
-
-def last_kernel(inner, own, outer, rhi, rlo, out):
-    out[...] = row_blur(inner[...], own[...], outer[...], rhi[...], rlo[...])
-
-
-def assemble_kernel(depth, *refs):
-    early, late, out = refs[:VIEWS], refs[VIEWS : 2 * VIEWS], refs[2 * VIEWS]
-    for slot in range(VIEWS):
-        value = late[slot][...] + pick(lax.rem(depth[0] + 3 - slot, 3), [r[...] for r in early])
-        out[0, slot, 0] = value[:ROWS]
-        out[1, slot, 0] = value[ROWS:]
+        give_out(slot[0], [r[...] for r in older] + [field], outs[2:])
+
+
+def last_kernel(which, inner, own, outer, *refs):
+    older, (rhi, rlo), outs = refs[: SLABS - 1], refs[SLABS - 1 : SLABS + 1], refs[SLABS + 1 :]
+    field = row_blur(inner[...], own[...], outer[...], rhi[...], rlo[...])
+    give_out(which[0], [r[...] for r in older] + [field], outs)
 
 
 FIELD = jax.ShapeDtypeStruct((2 * ROWS, COLS), jnp.float32)
 PAIR = jax.ShapeDtypeStruct((2, 2 * ROWS, COLS), jnp.float32)
 
 
-def call(kernel, out_shape, args, scalars=0, hbm=(), out_hbm=False):
+def assemble_kernel(depth, *refs):
+    received, out = refs[:-1], refs[-1]
+    for j in range(SLABS):
+
+        @pl.when(depth[0] == j)
+        def _():
+            for k in range(VIEWS):
+                (n,) = [n for n, give in enumerate(GIVES) if give.get(k) == j]
+                value = received[n][...]
+                out[0, k, 0] = value[:ROWS]
+                out[1, k, 0] = value[ROWS:]
+
+
+def call(kernel, out_shape, args, scalars=0, hbm=(), out_hbm=False, grant=16 << 20):
     vmem, smem = pl.BlockSpec(memory_space=pltpu.VMEM), pl.BlockSpec(memory_space=pltpu.SMEM)
     specs, held = [], []
     for i, arg in enumerate(args):
@@ -201,7 +271,11 @@
         held.append(arg if scalar or i in hbm else pltpu.with_memory_space_constraint(arg, pltpu.VMEM))
     shapes = out_shape if out_hbm else jax.tree.map(lambda s: pltpu.VMEM(s.shape, s.dtype), out_shape)
     return pl.pallas_call(
-        kernel, out_shape=shapes, in_specs=specs, out_specs=jax.tree.map(lambda _: vmem, out_shape)
+        kernel,
+        out_shape=shapes,
+        in_specs=specs,
+        out_specs=jax.tree.map(lambda _: vmem, out_shape),
+        compiler_params=pltpu.CompilerParams(vmem_limit_bytes=grant),
     )(*held)
 
 
@@ -212,9 +286,10 @@
 def propagate(incident, delta, beta, view_order):
     depth, tile = lax.axis_index("depth"), lax.axis_index("tile")
     chip_z, x_lo = tile % 8, tile // 32
-    slot = jnp.minimum((depth // 2) * 2 + chip_z // 4, VIEWS - 1)
+    quarter = (depth // 2) * 2 + chip_z // 4
+    slot = jnp.minimum(quarter, VIEWS - 1)
     row_z = jnp.where(depth % 2 == 0, chip_z, 7 - chip_z)
-    row_y = jnp.where(x_lo == 0, tile % 32 // 8, 3 - tile % 32 // 8)
+    row_y = jnp.where(x_lo == flipped(quarter), 3 - tile % 32 // 8, tile % 32 // 8)
     place = x_lo * 32 + row_y * 8 + row_z
 
     chi, clo = halves(column_matrix())
@@ -225,58 +300,54 @@
     rhi = jnp.where(keep, jnp.where(place % 2 == 0, ehi, ohi), 0)
     rlo = jnp.where(keep, jnp.where(place % 2 == 0, elo, olo), 0)
 
-    sent = call(
+    rest = call(
         prepare_kernel,
-        [FIELD] * (2 * VIEWS) + [PAIR] * VIEWS,
+        [PAIR] * SLABS + [FIELD] * len(FIRST),
         (view_order, depth[None], incident, delta, beta),
         scalars=2,
         hbm=(2, 3, 4),
+        grant=None,
     )
-    entering, second, rest = sent[:VIEWS], sent[VIEWS : 2 * VIEWS], sent[2 * VIEWS :]
-
-    def from_first(values):
-        return [permute(values[k], [(home(0, p), worker(k, p)) for p in range(TILES)]) for k in range(VIEWS)]
-
-    starts = from_first(entering)
-    seconds = from_first(second)
-    later = [
-        permute(rest[m], [(home(1 + (m + k) % 3, p), worker(k, p)) for k in range(VIEWS) for p in range(TILES)])
-        for m in range(3)
-    ]
-    own = call(first_kernel, FIELD, (*starts, chi, clo))
-    slabs = []
+    trans = []
+    for m in range(SLABS):
+        pairs = [(home((m - turn(k)) % SLABS, p), worker(k, p)) for k in range(VIEWS) for p in range(TILES)]
+        trans.append(permute(rest[m], completed(pairs)))
+
+    fields = [trans[turn(k)] for k in range(VIEWS)]
+    for k, value in zip(FIRST, rest[SLABS:]):
+        fields[k] = permute(value, [(home(0, p), worker(k, p)) for p in range(TILES)])
+
+    own = call(first_kernel, FIELD, (slot[None], *fields, chi, clo), scalars=1)
+    slabs, received = [], []
     for piece in range(2 * SLABS):
         inner = permute(own, INNER)
         outer = permute(own, OUTER)
-        if piece == 2 * SLABS - 1:
-            slabs.append(call(last_kernel, FIELD, (inner, own, outer, rhi, rlo)))
-            break
-        slab_end = piece % 2 == 1
         nxt = piece + 1
-        if nxt == 1:
-            t, half, which = seconds, None, slot
+        if nxt < 2 * SLABS:
+            leaving = len(ready(piece // 2)) if piece % 2 else -1
+            outs = call(
+                functools.partial(middle_kernel, piece),
+                [FIELD] * (2 + leaving),
+                (slot[None], inner, own, outer, *(slabs if piece % 2 else ()), *trans, rhi, rlo, chi, clo),
+                scalars=1,
+            )
+            own, outs = outs[0], outs[1:]
+            if piece % 2:
+                slabs.append(outs[0])
+                outs = outs[1:]
         else:
-            t, half, which = later, nxt % 2, (nxt // 2 + 5 - slot) % 3
-        outs = call(
-            functools.partial(middle_kernel, slab_end, half),
-            [FIELD] * (2 if slab_end else 1),
-            (which[None], inner, own, outer, *t, rhi, rlo, chi, clo),
-            scalars=1,
-        )
-        own = outs[0]
-        if slab_end:
-            slabs.append(outs[1])
-
-    early = [
-        permute(
-            pick((slot + n) % 3, slabs[:3]),
-            [(worker(k, p), home((n + k) % 3, p)) for k in range(VIEWS) for p in range(TILES)],
-        )
-        for n in range(3)
-    ]
-    late = [permute(slabs[3], [(worker(k, p), home(SLABS - 1, p)) for p in range(TILES)]) for k in range(VIEWS)]
+            outs = call(
+                last_kernel,
+                [FIELD] * len(ready(SLABS - 1)),
+                (slot[None], inner, own, outer, *slabs, rhi, rlo),
+                scalars=1,
+            )
+        for value in outs:
+            n = len(received)
+            pairs = [(worker(k, p), home(j, p)) for k, j in GIVES[n].items() for p in range(TILES)]
+            received.append(permute(value, completed(pairs)))
     shape = jax.ShapeDtypeStruct((2, VIEWS, 1, ROWS, COLS), jnp.float32)
-    return call(assemble_kernel, shape, (depth[None], *early, *late), scalars=1, out_hbm=True)
+    return call(assemble_kernel, shape, (depth[None], *received), scalars=1, out_hbm=True)
 
 
 def solution(mesh):

time: 119 us -> 116 us (0.975)
  the two profiles are of different devices: /device:TPU:71 before, /device:TPU:37 now
where the time goes in v3:
time: 116 us
  starting transfers between devices  70.6 us (61%)
  waiting for transfers between devices  36.9 us (32%)
  Pallas kernels  7.71 us (7%)
    ppermute x28, starting transfers between devices, permute(): return lax.ppermute(value, AXES, pairs)  70.6 us
    ppermute x28, waiting for transfers between devices, permute(): return lax.ppermute(value, AXES, pairs)  36.9 us
    pallas_call x11, Pallas kernels, call(): pl.pallas_call(kernel, out_shape=shapes, in_specs=specs, out_specs=jax.tr...  7.71 us
  transfers between devices with their start and end apart: 28, of which 15 were waited for; matrix products, arithmetic and copies ran while one was open for 0% of the time, Pallas kernels for 1%

profile of v3, /device:TPU:37, one launch (start us, length us, event | category | flops | bytes accessed | tf_op | source)
XLA Modules:
  0.0 115.8 jit_solution(2316842257163174978)
XLA Ops:
  0.0 1.8 %shard_map.73 = (f32[2,64,512]{2,1,0:T(8,128)S(1)}, f32[2,64,512]{2,1,0:T(8,128)S(1)}, f32[2,64,512]{2,1,0:T(8,128)S(1)}, f32[2,64,512]{2,1,0:T(8,128)S(1)}, f32...) custom-call(s32[3]{0:T(128)} %order.1, s32[1]{0:T(128)} %bitcast.depth, f32[2,3,32,512]{3,2,1,0:T(8,128)} %incident.1, ...), custom_call_target="tpu_custom_call" | custom-call | tf_op jit(solution)/shard_map/pallas_call | solution.py:273
  1.8 0.9 collective-permute-start.2
  2.8 0.7 collective-permute-start
  3.4 0.7 collective-permute-start.1
  4.1 12.1 %collective-permute-start.5 = (f32[2,64,512]{2,1,0:T(8,128)S(1)}, f32[2,64,512]{2,1,0:T(8,128)S(1)}, u32[]{:S(2)}, u32[]{:S(2)}) collective-permute-start(f32[2,64,512]{2,1,0:T(8,128)S(1)} %get-tuple-element.26), channel_id=1, source_target_pairs={{0,0},{1,1},{2,2},{3,3},{4,67},{5,66},{6,65},{7,64},{8,8},{9,9},{1... | collective-permute-start | bytes 786440 | tf_op jit(solution)/shard_map/ppermute | solution.py:283
  16.2 1.9 %collective-permute-start.6 = (f32[2,64,512]{2,1,0:T(8,128)S(1)}, f32[2,64,512]{2,1,0:T(8,128)S(1)}, u32[]{:S(2)}, u32[]{:S(2)}) collective-permute-start(f32[2,64,512]{2,1,0:T(8,128)S(1)} %get-tuple-element.27), channel_id=1, source_target_pairs={{64,0},{65,1},{66,2},{67,3},{68,67},{69,66},{70,65},{71,64},{72,8}... | collective-permute-start | bytes 786440 | tf_op jit(solution)/shard_map/ppermute | solution.py:283
  18.5 0.4 shard_map.74.own
  18.9 0.8 collective-permute-start.4
  19.8 6.8 %collective-permute-start.3 = (f32[64,512]{1,0:T(8,128)S(1)}, f32[64,512]{1,0:T(8,128)S(1)}, u32[]{:S(2)}, u32[]{:S(2)}) collective-permute-start(f32[64,512]{1,0:T(8,128)S(1)} %shard_map.74.own), channel_id=1, source_target_pairs={{0,1},{1,0},{2,3},{3,2},{67,66},{66,67},{65,64},{64,65},{8,9},{9,8... | collective-permute-start | bytes 393224 | tf_op jit(solution)/shard_map/ppermute | solution.py:283
  26.6 2.0 %collective-permute-done.6.refs_2_.refs_3_.refs_4_ = f32[2,64,512]{2,1,0:T(8,128)S(1)} collective-permute-done((f32[2,64,512]{2,1,0:T(8,128)S(1)}, f32[2,64,512]{2,1,0:T(8,128)S(1)}, u32[]{:S(2)}, u32[]{:S(2)}) %collective-permute-start.6) | collective-permute-done | bytes 262176 | tf_op jit(solution)/shard_map/ppermute | solution.py:283
  28.6 2.6 %collective-permute-done.7.refs_3_.refs_4_.refs_5_ = f32[2,64,512]{2,1,0:T(8,128)S(1)} collective-permute-done((f32[2,64,512]{2,1,0:T(8,128)S(1)}, f32[2,64,512]{2,1,0:T(8,128)S(1)}, u32[]{:S(2)}, u32[]{:S(2)}) %collective-permute-start.7) | collective-permute-done | bytes 262176 | tf_op jit(solution)/shard_map/ppermute | solution.py:283
  31.3 4.4 %collective-permute-done.3.inner = f32[64,512]{1,0:T(8,128)S(1)} collective-permute-done((f32[64,512]{1,0:T(8,128)S(1)}, f32[64,512]{1,0:T(8,128)S(1)}, u32[]{:S(2)}, u32[]{:S(2)}) %collective-permute-start.3) | collective-permute-done | bytes 131104 | tf_op jit(solution)/shard_map/ppermute | solution.py:283
  35.7 0.6 shard_map.75.own
  36.3 0.8 collective-permute-start.9
  37.2 1.2 %collective-permute-start.8 = (f32[64,512]{1,0:T(8,128)S(1)}, f32[64,512]{1,0:T(8,128)S(1)}, u32[]{:S(2)}, u32[]{:S(2)}) collective-permute-start(f32[64,512]{1,0:T(8,128)S(1)} %shard_map.75.own), channel_id=1, source_target_pairs={{0,1},{1,0},{2,3},{3,2},{67,66},{66,67},{65,64},{64,65},{8,9},{9,8... | collective-permute-start | bytes 393224 | tf_op jit(solution)/shard_map/ppermute | solution.py:283
  38.4 2.6 %collective-permute-done.9.outer = f32[64,512]{1,0:T(8,128)S(1)} collective-permute-done((f32[64,512]{1,0:T(8,128)S(1)}, f32[64,512]{1,0:T(8,128)S(1)}, u32[]{:S(2)}, u32[]{:S(2)}) %collective-permute-start.9) | collective-permute-done | bytes 131104 | tf_op jit(solution)/shard_map/ppermute | solution.py:283
  41.0 0.5 collective-permute-done.8.inner
  41.5 0.6 shard_map.76
  42.2 0.8 collective-permute-start.11
  43.0 2.8 %collective-permute-start.10 = (f32[64,512]{1,0:T(8,128)S(1)}, f32[64,512]{1,0:T(8,128)S(1)}, u32[]{:S(2)}, u32[]{:S(2)}) collective-permute-start(f32[64,512]{1,0:T(8,128)S(1)} %get-tuple-element.29.own), channel_id=1, source_target_pairs={{0,1},{1,0},{2,3},{3,2},{67,66},{66,67},{65,64},{64,65},{8,9},{9,8... | collective-permute-start | bytes 393224 | tf_op jit(solution)/shard_map/ppermute | solution.py:283
  45.7 0.3 collective-permute-done.11.outer
  46.1 2.7 %collective-permute-done.10.inner = f32[64,512]{1,0:T(8,128)S(1)} collective-permute-done((f32[64,512]{1,0:T(8,128)S(1)}, f32[64,512]{1,0:T(8,128)S(1)}, u32[]{:S(2)}, u32[]{:S(2)}) %collective-permute-start.10) | collective-permute-done | bytes 131104 | tf_op jit(solution)/shard_map/ppermute | solution.py:283
  48.8 0.6 shard_map.77.own
  49.5 2.8 %collective-permute-start.12 = (f32[64,512]{1,0:T(8,128)S(1)}, f32[64,512]{1,0:T(8,128)S(1)}, u32[]{:S(2)}, u32[]{:S(2)}) collective-permute-start(f32[64,512]{1,0:T(8,128)S(1)} %shard_map.77.own), channel_id=1, source_target_pairs={{0,1},{1,0},{2,3},{3,2},{67,66},{66,67},{65,64},{64,65},{8,9},{9,8... | collective-permute-start | bytes 393224 | tf_op jit(solution)/shard_map/ppermute | solution.py:283
  52.4 1.0 collective-permute-done.13.outer
  53.4 2.0 %collective-permute-done.12.inner = f32[64,512]{1,0:T(8,128)S(1)} collective-permute-done((f32[64,512]{1,0:T(8,128)S(1)}, f32[64,512]{1,0:T(8,128)S(1)}, u32[]{:S(2)}, u32[]{:S(2)}) %collective-permute-start.12) | collective-permute-done | bytes 131104 | tf_op jit(solution)/shard_map/ppermute | solution.py:283
  55.3 0.6 shard_map.78
  56.1 3.1 %collective-permute-start.16 = (f32[64,512]{1,0:T(8,128)S(1)}, f32[64,512]{1,0:T(8,128)S(1)}, u32[]{:S(2)}, u32[]{:S(2)}) collective-permute-start(f32[64,512]{1,0:T(8,128)S(1)} %get-tuple-element.33.own), channel_id=1, source_target_pairs={{0,1},{1,0},{2,3},{3,2},{67,66},{66,67},{65,64},{64,65},{8,9},{9,8... | collective-permute-start | bytes 393224 | tf_op jit(solution)/shard_map/ppermute | solution.py:283
  59.2 0.7 collective-permute-done.17.outer
  59.9 2.6 %collective-permute-done.16.inner = f32[64,512]{1,0:T(8,128)S(1)} collective-permute-done((f32[64,512]{1,0:T(8,128)S(1)}, f32[64,512]{1,0:T(8,128)S(1)}, u32[]{:S(2)}, u32[]{:S(2)}) %collective-permute-start.16) | collective-permute-done | bytes 131104 | tf_op jit(solution)/shard_map/ppermute | solution.py:283
  62.5 0.6 shard_map.79.own
  63.2 2.5 %collective-permute-start.18 = (f32[64,512]{1,0:T(8,128)S(1)}, f32[64,512]{1,0:T(8,128)S(1)}, u32[]{:S(2)}, u32[]{:S(2)}) collective-permute-start(f32[64,512]{1,0:T(8,128)S(1)} %shard_map.79.own), channel_id=1, source_target_pairs={{0,1},{1,0},{2,3},{3,2},{67,66},{66,67},{65,64},{64,65},{8,9},{9,8... | collective-permute-start | bytes 393224 | tf_op jit(solution)/shard_map/ppermute | solution.py:283
  65.7 1.3 %collective-permute-done.19.outer = f32[64,512]{1,0:T(8,128)S(1)} collective-permute-done((f32[64,512]{1,0:T(8,128)S(1)}, f32[64,512]{1,0:T(8,128)S(1)}, u32[]{:S(2)}, u32[]{:S(2)}) %collective-permute-start.19) | collective-permute-done | bytes 131104 | tf_op jit(solution)/shard_map/ppermute | solution.py:283
  67.0 1.3 %collective-permute-done.18.inner = f32[64,512]{1,0:T(8,128)S(1)} collective-permute-done((f32[64,512]{1,0:T(8,128)S(1)}, f32[64,512]{1,0:T(8,128)S(1)}, u32[]{:S(2)}, u32[]{:S(2)}) %collective-permute-start.18) | collective-permute-done | bytes 131104 | tf_op jit(solution)/shard_map/ppermute | solution.py:283
  68.3 0.6 shard_map.80
  69.0 0.5 collective-permute-start.22
  69.5 4.0 %collective-permute-start.21 = (f32[64,512]{1,0:T(8,128)S(1)}, f32[64,512]{1,0:T(8,128)S(1)}, u32[]{:S(2)}, u32[]{:S(2)}) collective-permute-start(f32[64,512]{1,0:T(8,128)S(1)} %get-tuple-element.36.own), channel_id=1, source_target_pairs={{0,1},{1,0},{2,3},{3,2},{67,66},{66,67},{65,64},{64,65},{8,9},{9,8... | collective-permute-start | bytes 393224 | tf_op jit(solution)/shard_map/ppermute | solution.py:283
  73.5 3.6 %collective-permute-done.21.inner = f32[64,512]{1,0:T(8,128)S(1)} collective-permute-done((f32[64,512]{1,0:T(8,128)S(1)}, f32[64,512]{1,0:T(8,128)S(1)}, u32[]{:S(2)}, u32[]{:S(2)}) %collective-permute-start.21) | collective-permute-done | bytes 131104 | tf_op jit(solution)/shard_map/ppermute | solution.py:283
  77.1 0.6 shard_map.81.own
  77.9 2.8 %collective-permute-start.23 = (f32[64,512]{1,0:T(8,128)S(1)}, f32[64,512]{1,0:T(8,128)S(1)}, u32[]{:S(2)}, u32[]{:S(2)}) collective-permute-start(f32[64,512]{1,0:T(8,128)S(1)} %shard_map.81.own), channel_id=1, source_target_pairs={{0,1},{1,0},{2,3},{3,2},{67,66},{66,67},{65,64},{64,65},{8,9},{9,8... | collective-permute-start | bytes 393224 | tf_op jit(solution)/shard_map/ppermute | solution.py:283
  80.7 0.7 collective-permute-start.14
  81.4 13.4 %collective-permute-start.15 = (f32[64,512]{1,0:T(8,128)S(1)}, f32[64,512]{1,0:T(8,128)S(1)}, u32[]{:S(2)}, u32[]{:S(2)}) collective-permute-start(f32[64,512]{1,0:T(8,128)S(1)} %get-tuple-element.32), channel_id=1, source_target_pairs={{95,0},{94,1},{93,2},{92,3},{28,4},{29,5},{30,6},{31,7},{87,8},{86... | collective-permute-start | bytes 393224 | tf_op jit(solution)/shard_map/ppermute | solution.py:283
  94.7 1.9 %collective-permute-start.20 = (f32[64,512]{1,0:T(8,128)S(1)}, f32[64,512]{1,0:T(8,128)S(1)}, u32[]{:S(2)}, u32[]{:S(2)}) collective-permute-start(f32[64,512]{1,0:T(8,128)S(1)} %get-tuple-element.35), channel_id=1, source_target_pairs={{128,0},{129,1},{130,2},{131,3},{195,4},{194,5},{193,6},{192,7},{1... | collective-permute-start | bytes 393224 | tf_op jit(solution)/shard_map/ppermute | solution.py:283
  96.7 0.3 shard_map.82
  96.9 6.7 %collective-permute-start.25 = (f32[64,512]{1,0:T(8,128)S(1)}, f32[64,512]{1,0:T(8,128)S(1)}, u32[]{:S(2)}, u32[]{:S(2)}) collective-permute-start(f32[64,512]{1,0:T(8,128)S(1)} %get-tuple-element.38), channel_id=1, source_target_pairs={{0,192},{1,193},{2,194},{3,195},{67,196},{66,197},{65,198},{64,199... | collective-permute-start | bytes 393224 | tf_op jit(solution)/shard_map/ppermute | solution.py:283
  103.7 2.2 %collective-permute-start.27 = (f32[64,512]{1,0:T(8,128)S(1)}, f32[64,512]{1,0:T(8,128)S(1)}, u32[]{:S(2)}, u32[]{:S(2)}) collective-permute-start(f32[64,512]{1,0:T(8,128)S(1)} %get-tuple-element.40), channel_id=1, source_target_pairs={{128,192},{129,193},{130,194},{131,195},{195,196},{194,197},{193,1... | collective-permute-start | bytes 393224 | tf_op jit(solution)/shard_map/ppermute | solution.py:283
  105.9 9.1 %collective-permute-done.26.refs_4_ = f32[64,512]{1,0:T(8,128)S(1)} collective-permute-done((f32[64,512]{1,0:T(8,128)S(1)}, f32[64,512]{1,0:T(8,128)S(1)}, u32[]{:S(2)}, u32[]{:S(2)}) %collective-permute-start.26) | collective-permute-done | bytes 131104 | tf_op jit(solution)/shard_map/ppermute | solution.py:283
  115.0 0.8 shard_map.83
  (33 shorter events, 0.6 us)
Async XLA Ops:
  0.0 18.5 %copy-start.1 = (bf16[384,256]{1,0:T(8,128)(2,1)S(1)}, bf16[384,256]{1,0:T(8,128)(2,1)}, u32[]{:S(2)}) copy-start(bf16[384,256]{1,0:T(8,128)(2,1)} %constant.116.refs_3_.refs_6_.refs_7_.refs_8_) | copy-start | bytes 589828
  1.8 16.7 %copy-start = (bf16[384,256]{1,0:T(8,128)(2,1)S(1)}, bf16[384,256]{1,0:T(8,128)(2,1)}, u32[]{:S(2)}) copy-start(bf16[384,256]{1,0:T(8,128)(2,1)} %constant.119.refs_4_.refs_7_.refs_8_.refs_9_) | copy-start | bytes 589828
  1.8 16.6 %collective-permute-start.2 = (f32[2,64,512]{2,1,0:T(8,128)S(1)}, f32[2,64,512]{2,1,0:T(8,128)S(1)}, u32[]{:S(2)}, u32[]{:S(2)}) collective-permute-start(f32[2,64,512]{2,1,0:T(8,128)S(1)} %get-tuple-element.25), channel_id=1, source_target_pairs={{192,0},{193,1},{194,2},{195,3},{196,67},{197,66},{198,65},{199,64... | collective-permute-start | bytes 786440 | tf_op jit(solution)/shard_map/ppermute | solution.py:283
  2.8 15.5 %collective-permute-start = (f32[64,512]{1,0:T(8,128)S(1)}, f32[64,512]{1,0:T(8,128)S(1)}, u32[]{:S(2)}, u32[]{:S(2)}) collective-permute-start(f32[64,512]{1,0:T(8,128)S(1)} %get-tuple-element.23), channel_id=1, source_target_pairs={{0,0},{1,1},{2,2},{3,3},{4,67},{5,66},{6,65},{7,64},{8,8},{9,9},{1... | collective-permute-start | bytes 393224 | tf_op jit(solution)/shard_map/ppermute | solution.py:283
  3.4 15.0 %collective-permute-start.1 = (f32[64,512]{1,0:T(8,128)S(1)}, f32[64,512]{1,0:T(8,128)S(1)}, u32[]{:S(2)}, u32[]{:S(2)}) collective-permute-start(f32[64,512]{1,0:T(8,128)S(1)} %get-tuple-element.24), channel_id=1, source_target_pairs={{0,95},{1,94},{2,93},{3,92},{4,28},{5,29},{6,30},{7,31},{8,87},{9,... | collective-permute-start | bytes 393224 | tf_op jit(solution)/shard_map/ppermute | solution.py:283
  4.1 22.5 %collective-permute-start.5 = (f32[2,64,512]{2,1,0:T(8,128)S(1)}, f32[2,64,512]{2,1,0:T(8,128)S(1)}, u32[]{:S(2)}, u32[]{:S(2)}) collective-permute-start(f32[2,64,512]{2,1,0:T(8,128)S(1)} %get-tuple-element.26), channel_id=1, source_target_pairs={{0,0},{1,1},{2,2},{3,3},{4,67},{5,66},{6,65},{7,64},{8,8},{9,9},{1... | collective-permute-start | bytes 786440 | tf_op jit(solution)/shard_map/ppermute | solution.py:283
  16.2 12.4 %collective-permute-start.6 = (f32[2,64,512]{2,1,0:T(8,128)S(1)}, f32[2,64,512]{2,1,0:T(8,128)S(1)}, u32[]{:S(2)}, u32[]{:S(2)}) collective-permute-start(f32[2,64,512]{2,1,0:T(8,128)S(1)} %get-tuple-element.27), channel_id=1, source_target_pairs={{64,0},{65,1},{66,2},{67,3},{68,67},{69,66},{70,65},{71,64},{72,8}... | collective-permute-start | bytes 786440 | tf_op jit(solution)/shard_map/ppermute | solution.py:283
  18.3 13.0 %collective-permute-start.7 = (f32[2,64,512]{2,1,0:T(8,128)S(1)}, f32[2,64,512]{2,1,0:T(8,128)S(1)}, u32[]{:S(2)}, u32[]{:S(2)}) collective-permute-start(f32[2,64,512]{2,1,0:T(8,128)S(1)} %get-tuple-element.28), channel_id=1, source_target_pairs={{128,0},{129,1},{130,2},{131,3},{132,67},{133,66},{134,65},{135,64... | collective-permute-start | bytes 786440 | tf_op jit(solution)/shard_map/ppermute | solution.py:283
  18.5 8.1 %copy-start.2 = (bf16[64,192]{1,0:T(8,128)(2,1)S(1)}, bf16[64,192]{1,0:T(8,128)(2,1)}, u32[]{:S(2)}) copy-start(bf16[64,192]{1,0:T(8,128)(2,1)} %constant.127) | copy-start | bytes 73732
  18.5 8.1 %copy-start.3 = (bf16[64,192]{1,0:T(8,128)(2,1)S(1)}, bf16[64,192]{1,0:T(8,128)(2,1)}, u32[]{:S(2)}) copy-start(bf16[64,192]{1,0:T(8,128)(2,1)} %constant.124) | copy-start | bytes 73732
  18.5 8.1 %copy-start.4 = (bf16[64,192]{1,0:T(8,128)(2,1)S(1)}, bf16[64,192]{1,0:T(8,128)(2,1)}, u32[]{:S(2)}) copy-start(bf16[64,192]{1,0:T(8,128)(2,1)} %constant.121) | copy-start | bytes 73732
  18.5 8.1 %copy-start.5 = (bf16[64,192]{1,0:T(8,128)(2,1)S(1)}, bf16[64,192]{1,0:T(8,128)(2,1)}, u32[]{:S(2)}) copy-start(bf16[64,192]{1,0:T(8,128)(2,1)} %constant.120) | copy-start | bytes 73732
  18.9 12.3 %collective-permute-start.4 = (f32[64,512]{1,0:T(8,128)S(1)}, f32[64,512]{1,0:T(8,128)S(1)}, u32[]{:S(2)}, u32[]{:S(2)}) collective-permute-start(f32[64,512]{1,0:T(8,128)S(1)} %shard_map.74.own), channel_id=1, source_target_pairs={{0,96},{1,2},{2,1},{3,67},{67,3},{66,65},{65,66},{64,8},{8,64},{9,... | collective-permute-start | bytes 393224 | tf_op jit(solution)/shard_map/ppermute | solution.py:283
  19.8 15.9 %collective-permute-start.3 = (f32[64,512]{1,0:T(8,128)S(1)}, f32[64,512]{1,0:T(8,128)S(1)}, u32[]{:S(2)}, u32[]{:S(2)}) collective-permute-start(f32[64,512]{1,0:T(8,128)S(1)} %shard_map.74.own), channel_id=1, source_target_pairs={{0,1},{1,0},{2,3},{3,2},{67,66},{66,67},{65,64},{64,65},{8,9},{9,8... | collective-permute-start | bytes 393224 | tf_op jit(solution)/shard_map/ppermute | solution.py:283
  36.3 4.7 %collective-permute-start.9 = (f32[64,512]{1,0:T(8,128)S(1)}, f32[64,512]{1,0:T(8,128)S(1)}, u32[]{:S(2)}, u32[]{:S(2)}) collective-permute-start(f32[64,512]{1,0:T(8,128)S(1)} %shard_map.75.own), channel_id=1, source_target_pairs={{0,96},{1,2},{2,1},{3,67},{67,3},{66,65},{65,66},{64,8},{8,64},{9,... | collective-permute-start | bytes 393224 | tf_op jit(solution)/shard_map/ppermute | solution.py:283
  37.2 4.4 %collective-permute-start.8 = (f32[64,512]{1,0:T(8,128)S(1)}, f32[64,512]{1,0:T(8,128)S(1)}, u32[]{:S(2)}, u32[]{:S(2)}) collective-permute-start(f32[64,512]{1,0:T(8,128)S(1)} %shard_map.75.own), channel_id=1, source_target_pairs={{0,1},{1,0},{2,3},{3,2},{67,66},{66,67},{65,64},{64,65},{8,9},{9,8... | collective-permute-start | bytes 393224 | tf_op jit(solution)/shard_map/ppermute | solution.py:283
  42.2 3.9 %collective-permute-start.11 = (f32[64,512]{1,0:T(8,128)S(1)}, f32[64,512]{1,0:T(8,128)S(1)}, u32[]{:S(2)}, u32[]{:S(2)}) collective-permute-start(f32[64,512]{1,0:T(8,128)S(1)} %get-tuple-element.29.own), channel_id=1, source_target_pairs={{0,96},{1,2},{2,1},{3,67},{67,3},{66,65},{65,66},{64,8},{8,64},{9,... | collective-permute-start | bytes 393224 | tf_op jit(solution)/shard_map/ppermute | solution.py:283
  43.0 5.8 %collective-permute-start.10 = (f32[64,512]{1,0:T(8,128)S(1)}, f32[64,512]{1,0:T(8,128)S(1)}, u32[]{:S(2)}, u32[]{:S(2)}) collective-permute-start(f32[64,512]{1,0:T(8,128)S(1)} %get-tuple-element.29.own), channel_id=1, source_target_pairs={{0,1},{1,0},{2,3},{3,2},{67,66},{66,67},{65,64},{64,65},{8,9},{9,8... | collective-permute-start | bytes 393224 | tf_op jit(solution)/shard_map/ppermute | solution.py:283
  49.4 3.9 %collective-permute-start.13 = (f32[64,512]{1,0:T(8,128)S(1)}, f32[64,512]{1,0:T(8,128)S(1)}, u32[]{:S(2)}, u32[]{:S(2)}) collective-permute-start(f32[64,512]{1,0:T(8,128)S(1)} %shard_map.77.own), channel_id=1, source_target_pairs={{0,96},{1,2},{2,1},{3,67},{67,3},{66,65},{65,66},{64,8},{8,64},{9,... | collective-permute-start | bytes 393224 | tf_op jit(solution)/shard_map/ppermute | solution.py:283
  49.5 5.8 %collective-permute-start.12 = (f32[64,512]{1,0:T(8,128)S(1)}, f32[64,512]{1,0:T(8,128)S(1)}, u32[]{:S(2)}, u32[]{:S(2)}) collective-permute-start(f32[64,512]{1,0:T(8,128)S(1)} %shard_map.77.own), channel_id=1, source_target_pairs={{0,1},{1,0},{2,3},{3,2},{67,66},{66,67},{65,64},{64,65},{8,9},{9,8... | collective-permute-start | bytes 393224 | tf_op jit(solution)/shard_map/ppermute | solution.py:283
  56.0 3.9 %collective-permute-start.17 = (f32[64,512]{1,0:T(8,128)S(1)}, f32[64,512]{1,0:T(8,128)S(1)}, u32[]{:S(2)}, u32[]{:S(2)}) collective-permute-start(f32[64,512]{1,0:T(8,128)S(1)} %get-tuple-element.33.own), channel_id=1, source_target_pairs={{0,96},{1,2},{2,1},{3,67},{67,3},{66,65},{65,66},{64,8},{8,64},{9,... | collective-permute-start | bytes 393224 | tf_op jit(solution)/shard_map/ppermute | solution.py:283
  56.1 6.4 %collective-permute-start.16 = (f32[64,512]{1,0:T(8,128)S(1)}, f32[64,512]{1,0:T(8,128)S(1)}, u32[]{:S(2)}, u32[]{:S(2)}) collective-permute-start(f32[64,512]{1,0:T(8,128)S(1)} %get-tuple-element.33.own), channel_id=1, source_target_pairs={{0,1},{1,0},{2,3},{3,2},{67,66},{66,67},{65,64},{64,65},{8,9},{9,8... | collective-permute-start | bytes 393224 | tf_op jit(solution)/shard_map/ppermute | solution.py:283
  63.1 3.9 %collective-permute-start.19 = (f32[64,512]{1,0:T(8,128)S(1)}, f32[64,512]{1,0:T(8,128)S(1)}, u32[]{:S(2)}, u32[]{:S(2)}) collective-permute-start(f32[64,512]{1,0:T(8,128)S(1)} %shard_map.79.own), channel_id=1, source_target_pairs={{0,96},{1,2},{2,1},{3,67},{67,3},{66,65},{65,66},{64,8},{8,64},{9,... | collective-permute-start | bytes 393224 | tf_op jit(solution)/shard_map/ppermute | solution.py:283
  63.2 5.1 %collective-permute-start.18 = (f32[64,512]{1,0:T(8,128)S(1)}, f32[64,512]{1,0:T(8,128)S(1)}, u32[]{:S(2)}, u32[]{:S(2)}) collective-permute-start(f32[64,512]{1,0:T(8,128)S(1)} %shard_map.79.own), channel_id=1, source_target_pairs={{0,1},{1,0},{2,3},{3,2},{67,66},{66,67},{65,64},{64,65},{8,9},{9,8... | collective-permute-start | bytes 393224 | tf_op jit(solution)/shard_map/ppermute | solution.py:283
  69.0 4.6 %collective-permute-start.22 = (f32[64,512]{1,0:T(8,128)S(1)}, f32[64,512]{1,0:T(8,128)S(1)}, u32[]{:S(2)}, u32[]{:S(2)}) collective-permute-start(f32[64,512]{1,0:T(8,128)S(1)} %get-tuple-element.36.own), channel_id=1, source_target_pairs={{0,96},{1,2},{2,1},{3,67},{67,3},{66,65},{65,66},{64,8},{8,64},{9,... | collective-permute-start | bytes 393224 | tf_op jit(solution)/shard_map/ppermute | solution.py:283
  69.5 7.6 %collective-permute-start.21 = (f32[64,512]{1,0:T(8,128)S(1)}, f32[64,512]{1,0:T(8,128)S(1)}, u32[]{:S(2)}, u32[]{:S(2)}) collective-permute-start(f32[64,512]{1,0:T(8,128)S(1)} %get-tuple-element.36.own), channel_id=1, source_target_pairs={{0,1},{1,0},{2,3},{3,2},{67,66},{66,67},{65,64},{64,65},{8,9},{9,8... | collective-permute-start | bytes 393224 | tf_op jit(solution)/shard_map/ppermute | solution.py:283
  77.8 18.9 %collective-permute-start.24 = (f32[64,512]{1,0:T(8,128)S(1)}, f32[64,512]{1,0:T(8,128)S(1)}, u32[]{:S(2)}, u32[]{:S(2)}) collective-permute-start(f32[64,512]{1,0:T(8,128)S(1)} %shard_map.81.own), channel_id=1, source_target_pairs={{0,96},{1,2},{2,1},{3,67},{67,3},{66,65},{65,66},{64,8},{8,64},{9,... | collective-permute-start | bytes 393224 | tf_op jit(solution)/shard_map/ppermute | solution.py:283
  77.9 18.8 %collective-permute-start.23 = (f32[64,512]{1,0:T(8,128)S(1)}, f32[64,512]{1,0:T(8,128)S(1)}, u32[]{:S(2)}, u32[]{:S(2)}) collective-permute-start(f32[64,512]{1,0:T(8,128)S(1)} %shard_map.81.own), channel_id=1, source_target_pairs={{0,1},{1,0},{2,3},{3,2},{67,66},{66,67},{65,64},{64,65},{8,9},{9,8... | collective-permute-start | bytes 393224 | tf_op jit(solution)/shard_map/ppermute | solution.py:283
  80.7 23.0 %collective-permute-start.14 = (f32[64,512]{1,0:T(8,128)S(1)}, f32[64,512]{1,0:T(8,128)S(1)}, u32[]{:S(2)}, u32[]{:S(2)}) collective-permute-start(f32[64,512]{1,0:T(8,128)S(1)} %get-tuple-element.31), channel_id=1, source_target_pairs={{0,0},{1,1},{2,2},{3,3},{67,4},{66,5},{65,6},{64,7},{8,8},{9,9},{1... | collective-permute-start | bytes 393224 | tf_op jit(solution)/shard_map/ppermute | solution.py:283
  81.4 24.6 %collective-permute-start.15 = (f32[64,512]{1,0:T(8,128)S(1)}, f32[64,512]{1,0:T(8,128)S(1)}, u32[]{:S(2)}, u32[]{:S(2)}) collective-permute-start(f32[64,512]{1,0:T(8,128)S(1)} %get-tuple-element.32), channel_id=1, source_target_pairs={{95,0},{94,1},{93,2},{92,3},{28,4},{29,5},{30,6},{31,7},{87,8},{86... | collective-permute-start | bytes 393224 | tf_op jit(solution)/shard_map/ppermute | solution.py:283
  94.7 11.2 %collective-permute-start.20 = (f32[64,512]{1,0:T(8,128)S(1)}, f32[64,512]{1,0:T(8,128)S(1)}, u32[]{:S(2)}, u32[]{:S(2)}) collective-permute-start(f32[64,512]{1,0:T(8,128)S(1)} %get-tuple-element.35), channel_id=1, source_target_pairs={{128,0},{129,1},{130,2},{131,3},{195,4},{194,5},{193,6},{192,7},{1... | collective-permute-start | bytes 393224 | tf_op jit(solution)/shard_map/ppermute | solution.py:283
  96.9 9.0 %collective-permute-start.25 = (f32[64,512]{1,0:T(8,128)S(1)}, f32[64,512]{1,0:T(8,128)S(1)}, u32[]{:S(2)}, u32[]{:S(2)}) collective-permute-start(f32[64,512]{1,0:T(8,128)S(1)} %get-tuple-element.38), channel_id=1, source_target_pairs={{0,192},{1,193},{2,194},{3,195},{67,196},{66,197},{65,198},{64,199... | collective-permute-start | bytes 393224 | tf_op jit(solution)/shard_map/ppermute | solution.py:283
  103.6 11.4 %collective-permute-start.26 = (f32[64,512]{1,0:T(8,128)S(1)}, f32[64,512]{1,0:T(8,128)S(1)}, u32[]{:S(2)}, u32[]{:S(2)}) collective-permute-start(f32[64,512]{1,0:T(8,128)S(1)} %get-tuple-element.39), channel_id=1, source_target_pairs={{95,192},{94,193},{93,194},{92,195},{28,196},{29,197},{30,198},{31... | collective-permute-start | bytes 393224 | tf_op jit(solution)/shard_map/ppermute | solution.py:283
  103.7 11.3 %collective-permute-start.27 = (f32[64,512]{1,0:T(8,128)S(1)}, f32[64,512]{1,0:T(8,128)S(1)}, u32[]{:S(2)}, u32[]{:S(2)}) collective-permute-start(f32[64,512]{1,0:T(8,128)S(1)} %get-tuple-element.40), channel_id=1, source_target_pairs={{128,192},{129,193},{130,194},{131,195},{195,196},{194,197},{193,1... | collective-permute-start | bytes 393224 | tf_op jit(solution)/shard_map/ppermute | solution.py:283
